TPU v7x, 32 devices: a whole 2x2x4 slice. The times are simulated.
32 devices in a mesh: dp: 8 (over y, x, core), stream: 4 (over z).
Axes of the slice: x: 2, y: 2, z: 4, core: 2. Of those that a mesh axis runs over, the one named last changes fastest.
Arguments:
- text_input: bfloat16 [64, 512, 768], P('dp', 'stream'), may hold values from -6 to 6
- visual_features: bfloat16 [64, 49, 256], P(('dp', 'stream')), may hold values from -6 to 6
- receipt_text: int32 [64, 512], P('dp'), may hold values from 0 to 7, never falling along the last dimension, each value on 1 to 128 neighbouring positions
- receipt_visual: int32 [64, 49], P('dp'), may hold values from 0 to 7
- boxes: int32 [2, 64, 561], P(None, 'dp'), may hold values from 0 to 1023
- w_query: bfloat16 [768, 768], replicated, may hold values from -0.21875 to 0.21875
- b_query: bfloat16 [768], replicated, may hold values from -3 to 3
- w_key: bfloat16 [768, 768], replicated, may hold values from -0.21875 to 0.21875
- w_value: bfloat16 [768, 768], replicated, may hold values from -0.21875 to 0.21875
- b_value: bfloat16 [768], replicated, may hold values from -3 to 3
- w_out: bfloat16 [768, 768], replicated, may hold values from -1.75 to 1.75
- b_out: bfloat16 [768], replicated, may hold values from -3 to 3
- gain_attn: bfloat16 [768], replicated, may hold values from 0.099609375 to 1.8984375
- shift_attn: bfloat16 [768], replicated, may hold values from -2 to 2
- w_up: bfloat16 [768, 3072], replicated, may hold values from -0.21875 to 0.21875
- b_up: bfloat16 [3072], replicated, may hold values from -3 to 3
- w_down: bfloat16 [3072, 768], replicated, may hold values from -0.109375 to 0.109375
- b_down: bfloat16 [768], replicated, may hold values from -3 to 3
- gain_ffn: bfloat16 [768], replicated, may hold values from 0.099609375 to 1.8984375
- shift_ffn: bfloat16 [768], replicated, may hold values from -2 to 2
- w_visual: bfloat16 [256, 768], replicated, may hold values from -0.375 to 0.375
- b_visual: bfloat16 [768], replicated, may hold values from -3 to 3
- table_line: bfloat16 [12, 32], replicated, may hold values from -4 to 4
- table_x: bfloat16 [12, 64], replicated, may hold values from -4 to 4
- table_y: bfloat16 [12, 64], replicated, may hold values from -4 to 4
- cotangent_text: bfloat16 [64, 512, 768], P('dp', 'stream'), may hold values from -6 to 6
- cotangent_visual: bfloat16 [64, 49, 768], P(('dp', 'stream')), may hold values from -6 to 6
Outputs:
- out_text: bfloat16 [64, 512, 768], P('dp', 'stream')
- out_visual: bfloat16 [64, 49, 768], P(('dp', 'stream'))
- grad_text: float32 [64, 512, 768], P('dp', 'stream')
- grad_features: float32 [64, 49, 256], P(('dp', 'stream'))
- grad_w_query: float32 [768, 768], P(('dp', 'stream'))
- grad_b_query: float32 [768], P(('dp', 'stream'))
- grad_w_key: float32 [768, 768], P(('dp', 'stream'))
- grad_w_value: float32 [768, 768], P(('dp', 'stream'))
- grad_b_value: float32 [768], P(('dp', 'stream'))
- grad_w_out: float32 [768, 768], P(('dp', 'stream'))
- grad_b_out: float32 [768], P(('dp', 'stream'))
- grad_gain_attn: float32 [768], P(('dp', 'stream'))
- grad_shift_attn: float32 [768], P(('dp', 'stream'))
- grad_w_up: float32 [768, 3072], P(('dp', 'stream'))
- grad_b_up: float32 [3072], P(('dp', 'stream'))
- grad_w_down: float32 [3072, 768], P(('dp', 'stream'))
- grad_b_down: float32 [768], P(('dp', 'stream'))
- grad_gain_ffn: float32 [768], P(('dp', 'stream'))
- grad_shift_ffn: float32 [768], P(('dp', 'stream'))
- grad_w_visual: float32 [256, 768], P(('dp', 'stream'))
- grad_b_visual: float32 [768], P(('dp', 'stream'))
- grad_table_line: float32 [12, 32], replicated
- grad_table_x: float32 [12, 64], replicated
- grad_table_y: float32 [12, 64], replicated
Inputs may be any that keep to these rules, and one draw needn't show every extreme that they name: `receipt_text`: receipt ids never fall along a row's text; each of the 8 receipts holds 1 to 128 text slots of the row, and one holds exactly 128.
All inputs are finite; a program needn't handle non-finite values.
Results may differ from a plain program's by a relative error of at most 0.015.
Values may be sent and summed in bfloat16 or wider, within the bound.
No kernel may reach another device: no remote copies, remote signals or barrier semaphores. Data moves between devices by JAX's collectives and lax.ppermute only.
A program may use at most 320 MiB of HBM per device.

v0:
```python
import math

import jax
import jax.numpy as jnp
from jax import lax
from jax.sharding import PartitionSpec as P

H = 12
NB1 = 32
NB2 = 64


reach_line = 128
reach_plane = 256


def thresholds(half, reach):
    exact = half // 2
    steps = half - exact
    return [
        int(math.floor(exact * (reach / exact) ** (power / steps) + 0.5))
        for power in range(1, steps)
    ]


def bucket(diff, count, reach):
    half = count // 2
    exact = half // 2
    dist = jnp.abs(diff)
    passed = jnp.zeros_like(dist)
    for limit in thresholds(half, reach):
        passed = passed + (dist >= limit).astype(jnp.int32)
    inner = jnp.where(dist < exact, dist, exact + passed)
    return inner + half * (diff > 0).astype(jnp.int32)


def layer_norm(values, gain, shift):
    centred = values - jnp.mean(values, axis=-1, keepdims=True)
    spread = jnp.mean(centred * centred, axis=-1, keepdims=True)
    return centred * lax.rsqrt(spread + 1e-05) * gain + shift


def gelu_exact(values):
    return jax.nn.gelu(values, approximate=False)


def one_hot(index, count):
    levels = jnp.arange(count, dtype=jnp.int32).reshape((count,) + (1,) * index.ndim)
    return (index[None] == levels).astype(jnp.bfloat16)


def tiles(query_pos, key_pos, query_box, key_box):
    line = bucket(key_pos[None, :] - query_pos[:, None], NB1, reach_line)
    across = bucket(key_box[0][:, None, :] - query_box[0][:, :, None], NB2, reach_plane)
    down = bucket(key_box[1][:, None, :] - query_box[1][:, :, None], NB2, reach_plane)
    return (one_hot(line, NB1), one_hot(across, NB2), one_hot(down, NB2))


def bias_of(marks, tables):
    line = jnp.einsum("nqk,hn->hqk", marks[0], tables[0], preferred_element_type=jnp.float32)
    plane = jnp.einsum("nbqk,hn->bhqk", marks[1], tables[1], preferred_element_type=jnp.float32)
    plane = plane + jnp.einsum(
        "nbqk,hn->bhqk", marks[2], tables[2], preferred_element_type=jnp.float32
    )
    return line[None] + plane


def masked_scores(query, keys, marks, tables, query_seg, key_seg):
    scale = 1.0 / math.sqrt(query.shape[-1])
    raw = jnp.einsum("bqhd,bkhd->bhqk", query, keys, preferred_element_type=jnp.float32) * scale
    raw = raw + bias_of(marks, tables)
    same = (query_seg[:, :, None] == key_seg[:, None, :])[:, None]
    return (raw, same)


def attend(query, keys, values, marks, tables, query_seg, key_seg):
    raw, same = masked_scores(query, keys, marks, tables, query_seg, key_seg)
    masked = jnp.where(same, raw, -1e30)
    peak = jnp.max(masked, axis=-1, keepdims=True)
    expo = jnp.exp(masked - peak)
    total = jnp.sum(expo, axis=-1, keepdims=True)
    shares = (expo / total).astype(jnp.bfloat16)
    context = jnp.einsum("bhqk,bkhd->bqhd", shares, values, preferred_element_type=jnp.float32)
    return (context, peak + jnp.log(total))


def attend_back(query, keys, values, marks, tables, query_seg, key_seg, log_total, grad_context):
    scale = 1.0 / math.sqrt(query.shape[-1])
    raw, same = masked_scores(query, keys, marks, tables, query_seg, key_seg)
    probs = jnp.where(same, jnp.exp(raw - log_total), 0.0)
    shares = probs.astype(jnp.bfloat16)
    grad_values = jnp.einsum(
        "bhqk,bqhd->bkhd", shares, grad_context, preferred_element_type=jnp.float32
    )
    grad_probs = jnp.einsum(
        "bqhd,bkhd->bhqk", grad_context, values, preferred_element_type=jnp.float32
    )
    inner = jnp.sum(probs * grad_probs, axis=-1, keepdims=True)
    grad_scores = (probs * (grad_probs - inner)).astype(jnp.bfloat16)
    grad_query = (
        jnp.einsum("bhqk,bkhd->bqhd", grad_scores, keys, preferred_element_type=jnp.float32) * scale
    )
    grad_keys = (
        jnp.einsum("bhqk,bqhd->bkhd", grad_scores, query, preferred_element_type=jnp.float32)
        * scale
    )
    grad_tables = (
        jnp.einsum("nqk,bhqk->hn", marks[0], grad_scores, preferred_element_type=jnp.float32),
        jnp.einsum("nbqk,bhqk->hn", marks[1], grad_scores, preferred_element_type=jnp.float32),
        jnp.einsum("nbqk,bhqk->hn", marks[2], grad_scores, preferred_element_type=jnp.float32),
    )
    return (grad_query, grad_keys, grad_values, grad_tables)


def in_blocks(values, count, dim):
    shape = values.shape
    grouped = values.reshape(shape[:dim] + (count, shape[dim] // count) + shape[dim + 1 :])
    return jnp.moveaxis(grouped, dim, 0)


def per_device(
    text_input,
    visual_features,
    receipt_text,
    receipt_visual,
    boxes,
    w_query,
    b_query,
    w_key,
    w_value,
    b_value,
    w_out,
    b_out,
    gain_attn,
    shift_attn,
    w_up,
    b_up,
    w_down,
    b_down,
    gain_ffn,
    shift_ffn,
    w_visual,
    b_visual,
    table_line,
    table_x,
    table_y,
    cotangent_text,
    cotangent_visual,
):
    floating = jnp.float32
    narrow = jnp.bfloat16
    rows, local_text, width = text_input.shape
    own_rows, visual, channels = visual_features.shape
    whole_text = receipt_text.shape[1]
    slots = whole_text + visual
    heads = H
    head_size = width // heads
    tables = (table_line, table_x, table_y)
    place = lax.axis_index("stream")
    first_row = place * own_rows
    first_slot = place * local_text
    text_count = rows * local_text
    key_pos = jnp.concatenate(
        [jnp.arange(whole_text, dtype=jnp.int32), jnp.arange(visual, dtype=jnp.int32)]
    )
    key_seg = jnp.concatenate([receipt_text, receipt_visual], axis=1)

    def split_heads(values):
        return values.reshape(values.shape[:-1] + (heads, head_size))

    visual_pre = jnp.einsum(
        "rvc,cd->rvd", visual_features, w_visual, preferred_element_type=floating
    ) + b_visual.astype(floating)

    def text_part(values):
        return values[:text_count].reshape(rows, local_text, width)

    def visual_part(values):
        return values[text_count:].reshape(own_rows, visual, width)

    text_flat = text_input.reshape(-1, width)
    entered = jnp.concatenate([text_flat, visual_pre.astype(narrow).reshape(-1, width)], axis=0)
    stream_in = jnp.concatenate([text_flat.astype(floating), visual_pre.reshape(-1, width)], axis=0)
    query_all = (
        jnp.dot(entered, w_query, preferred_element_type=floating) + b_query.astype(floating)
    ).astype(narrow)
    key_all = jnp.dot(entered, w_key, preferred_element_type=floating).astype(narrow)
    value_all = (
        jnp.dot(entered, w_value, preferred_element_type=floating) + b_value.astype(floating)
    ).astype(narrow)
    query_all, key_all, value_all = (query_all, key_all, value_all)
    keys_text, values_text = (
        lax.all_gather(text_part(key_all), "stream", axis=1, tiled=True),
        lax.all_gather(text_part(value_all), "stream", axis=1, tiled=True),
    )
    keys_seen, values_seen = (
        lax.all_gather(visual_part(key_all), "stream", axis=0, tiled=True),
        lax.all_gather(visual_part(value_all), "stream", axis=0, tiled=True),
    )
    keys_full = split_heads(jnp.concatenate([keys_text, keys_seen], axis=1))
    values_full = split_heads(jnp.concatenate([values_text, values_seen], axis=1))
    text_pos = first_slot + jnp.arange(local_text, dtype=jnp.int32)
    text_box = lax.dynamic_slice_in_dim(boxes, first_slot, local_text, 2)
    text_seg = lax.dynamic_slice_in_dim(receipt_text, first_slot, local_text, 1)
    block_rows = math.gcd(rows, max(1, 512 // local_text))
    count = rows // block_rows
    text_items = (
        in_blocks(split_heads(text_part(query_all)), count, 0),
        in_blocks(keys_full, count, 0),
        in_blocks(values_full, count, 0),
        in_blocks(text_box, count, 1),
        in_blocks(boxes, count, 1),
        in_blocks(text_seg, count, 0),
        in_blocks(key_seg, count, 0),
    )

    def text_forward(item):
        query, keys, values, query_box, key_box, query_seg, seg_keys = item
        marks = tiles(text_pos, key_pos, query_box, key_box)
        return attend(query, keys, values, marks, tables, query_seg, seg_keys)

    context_text, total_text = lax.map(text_forward, text_items)
    vis_query = split_heads(visual_part(query_all))
    vis_keys = lax.dynamic_slice_in_dim(keys_full, first_row, own_rows, 0)
    vis_values = lax.dynamic_slice_in_dim(values_full, first_row, own_rows, 0)
    vis_box = lax.dynamic_slice_in_dim(boxes[:, :, whole_text:], first_row, own_rows, 1)
    vis_key_box = lax.dynamic_slice_in_dim(boxes, first_row, own_rows, 1)
    vis_seg = lax.dynamic_slice_in_dim(receipt_visual, first_row, own_rows, 0)
    vis_key_seg = lax.dynamic_slice_in_dim(key_seg, first_row, own_rows, 0)
    vis_pos = jnp.arange(visual, dtype=jnp.int32)
    vis_marks = tiles(vis_pos, key_pos, vis_box, vis_key_box)
    context_vis, total_vis = attend(
        vis_query, vis_keys, vis_values, vis_marks, tables, vis_seg, vis_key_seg
    )
    context_low = jnp.concatenate(
        [context_text.reshape(-1, width), context_vis.reshape(-1, width)], axis=0
    ).astype(narrow)
    grad_outcome = jnp.concatenate(
        [
            cotangent_text.reshape(-1, width).astype(floating),
            cotangent_visual.reshape(-1, width).astype(floating),
        ],
        axis=0,
    )
    attended = jnp.dot(context_low, w_out, preferred_element_type=floating) + b_out.astype(floating)
    norm_one, back_one = jax.vjp(
        layer_norm, stream_in + attended, gain_attn.astype(floating), shift_attn.astype(floating)
    )
    hidden = norm_one.astype(narrow)
    inner_up = jnp.dot(hidden, w_up, preferred_element_type=floating) + b_up.astype(floating)
    active, back_gelu = jax.vjp(gelu_exact, inner_up)
    active_low = active.astype(narrow)
    branch = jnp.dot(active_low, w_down, preferred_element_type=floating) + b_down.astype(floating)
    outcome, back_two = jax.vjp(
        layer_norm, norm_one + branch, gain_ffn.astype(floating), shift_ffn.astype(floating)
    )
    grad_top, grad_gain_ffn, grad_shift_ffn = back_two(grad_outcome)
    grad_branch = grad_top.astype(narrow)
    grad_b_down = jnp.sum(grad_branch, axis=0, dtype=floating)
    grad_w_down = jnp.einsum("tf,td->fd", active_low, grad_branch, preferred_element_type=floating)
    grad_active = jnp.einsum("td,fd->tf", grad_branch, w_down, preferred_element_type=floating)
    grad_inner = back_gelu(grad_active)[0].astype(narrow)
    grad_b_up = jnp.sum(grad_inner, axis=0, dtype=floating)
    grad_w_up = jnp.einsum("td,tf->df", hidden, grad_inner, preferred_element_type=floating)
    grad_norm = grad_top + jnp.einsum(
        "tf,df->td", grad_inner, w_up, preferred_element_type=floating
    )
    grad_mid, grad_gain_attn, grad_shift_attn = back_one(grad_norm)
    grad_attended = grad_mid.astype(narrow)
    grad_b_out = jnp.sum(grad_attended, axis=0, dtype=floating)
    grad_w_out = jnp.einsum(
        "td,te->de", context_low, grad_attended, preferred_element_type=floating
    )
    grad_context = jnp.einsum(
        "te,de->td", grad_attended, w_out, preferred_element_type=floating
    ).astype(narrow)
    weight_terms = (
        grad_w_out,
        grad_b_out,
        grad_gain_attn,
        grad_shift_attn,
        grad_w_up,
        grad_b_up,
        grad_w_down,
        grad_b_down,
        grad_gain_ffn,
        grad_shift_ffn,
    )
    outcome, grad_mid, grad_context, middle_terms = (outcome, grad_mid, grad_context, weight_terms)
    out_text = text_part(outcome).astype(narrow)
    out_visual = visual_part(outcome).astype(narrow)
    back_items = text_items + (
        total_text,
        in_blocks(split_heads(text_part(grad_context)), count, 0),
    )

    def text_backward(item):
        query, keys, values, query_box, key_box, query_seg, seg_keys, log_total, grad_piece = item
        marks = tiles(text_pos, key_pos, query_box, key_box)
        return attend_back(
            query, keys, values, marks, tables, query_seg, seg_keys, log_total, grad_piece
        )

    grad_query_text, grad_keys_text, grad_values_text, tables_text = lax.map(
        text_backward, back_items
    )
    grad_query_vis, grad_keys_vis, grad_values_vis, tables_vis = attend_back(
        vis_query,
        vis_keys,
        vis_values,
        vis_marks,
        tables,
        vis_seg,
        vis_key_seg,
        total_vis,
        split_heads(visual_part(grad_context)),
    )

    def with_visual(text_terms, visual_terms):
        merged = text_terms.reshape(rows, slots, width)
        mine = lax.dynamic_slice_in_dim(merged, first_row, own_rows, 0) + visual_terms.reshape(
            own_rows, slots, width
        )
        return lax.dynamic_update_slice_in_dim(merged, mine, first_row, 0)

    key_terms = with_visual(grad_keys_text, grad_keys_vis)
    value_terms = with_visual(grad_values_text, grad_values_vis)
    key_text_sum, value_text_sum = (
        lax.psum_scatter(
            key_terms[:, :whole_text].astype(jnp.bfloat16),
            "stream",
            scatter_dimension=1,
            tiled=True,
        ).astype(jnp.float32),
        lax.psum_scatter(
            value_terms[:, :whole_text].astype(jnp.bfloat16),
            "stream",
            scatter_dimension=1,
            tiled=True,
        ).astype(jnp.float32),
    )
    key_vis_sum, value_vis_sum = (
        lax.psum_scatter(
            key_terms[:, whole_text:].astype(jnp.bfloat16),
            "stream",
            scatter_dimension=0,
            tiled=True,
        ).astype(jnp.float32),
        lax.psum_scatter(
            value_terms[:, whole_text:].astype(jnp.bfloat16),
            "stream",
            scatter_dimension=0,
            tiled=True,
        ).astype(jnp.float32),
    )
    grad_query = jnp.concatenate(
        [grad_query_text.reshape(-1, width), grad_query_vis.reshape(-1, width)], axis=0
    ).astype(narrow)
    grad_key = jnp.concatenate(
        [key_text_sum.reshape(-1, width), key_vis_sum.reshape(-1, width)], axis=0
    ).astype(narrow)
    grad_value = jnp.concatenate(
        [value_text_sum.reshape(-1, width), value_vis_sum.reshape(-1, width)], axis=0
    ).astype(narrow)
    grad_w_query = jnp.einsum("td,te->de", entered, grad_query, preferred_element_type=floating)
    grad_b_query = jnp.sum(grad_query, axis=0, dtype=floating)
    grad_w_key = jnp.einsum("td,te->de", entered, grad_key, preferred_element_type=floating)
    grad_w_value = jnp.einsum("td,te->de", entered, grad_value, preferred_element_type=floating)
    grad_b_value = jnp.sum(grad_value, axis=0, dtype=floating)
    grad_stream = grad_mid + jnp.einsum(
        "te,de->td", grad_query, w_query, preferred_element_type=floating
    )
    grad_stream = grad_stream + jnp.einsum(
        "te,de->td", grad_key, w_key, preferred_element_type=floating
    )
    grad_stream = grad_stream + jnp.einsum(
        "te,de->td", grad_value, w_value, preferred_element_type=floating
    )
    grad_stream, proj_terms = (
        grad_stream,
        (grad_w_query, grad_b_query, grad_w_key, grad_w_value, grad_b_value),
    )
    grad_text = text_part(grad_stream)
    grad_visual = visual_part(grad_stream).astype(narrow)
    line_terms = jnp.sum(tables_text[0], axis=0) + tables_vis[0]
    across_terms = jnp.sum(tables_text[1], axis=0) + tables_vis[1]
    down_terms = jnp.sum(tables_text[2], axis=0) + tables_vis[2]
    grad_w_visual = jnp.einsum(
        "rvc,rvd->cd", visual_features, grad_visual, preferred_element_type=floating
    )
    grad_b_visual = jnp.sum(grad_visual, axis=(0, 1), dtype=floating)
    grad_features = jnp.einsum(
        "rvd,cd->rvc", grad_visual, w_visual, preferred_element_type=floating
    )
    grad_table_line, grad_table_x, grad_table_y = lax.psum(
        (line_terms, across_terms, down_terms), ("dp", "stream")
    )
    (
        grad_w_out,
        grad_b_out,
        grad_gain_attn,
        grad_shift_attn,
        grad_w_up,
        grad_b_up,
        grad_w_down,
        grad_b_down,
        grad_gain_ffn,
        grad_shift_ffn,
    ) = middle_terms
    grad_w_query, grad_b_query, grad_w_key, grad_w_value, grad_b_value = proj_terms
    summed = (
        lax.psum_scatter(grad_w_query, ("dp", "stream"), scatter_dimension=0, tiled=True),
        lax.psum_scatter(grad_b_query, ("dp", "stream"), scatter_dimension=0, tiled=True),
        lax.psum_scatter(grad_w_key, ("dp", "stream"), scatter_dimension=0, tiled=True),
        lax.psum_scatter(grad_w_value, ("dp", "stream"), scatter_dimension=0, tiled=True),
        lax.psum_scatter(grad_b_value, ("dp", "stream"), scatter_dimension=0, tiled=True),
        lax.psum_scatter(grad_w_out, ("dp", "stream"), scatter_dimension=0, tiled=True),
        lax.psum_scatter(grad_b_out, ("dp", "stream"), scatter_dimension=0, tiled=True),
        lax.psum_scatter(grad_gain_attn, ("dp", "stream"), scatter_dimension=0, tiled=True),
        lax.psum_scatter(grad_shift_attn, ("dp", "stream"), scatter_dimension=0, tiled=True),
        lax.psum_scatter(grad_w_up, ("dp", "stream"), scatter_dimension=0, tiled=True),
        lax.psum_scatter(grad_b_up, ("dp", "stream"), scatter_dimension=0, tiled=True),
        lax.psum_scatter(grad_w_down, ("dp", "stream"), scatter_dimension=0, tiled=True),
        lax.psum_scatter(grad_b_down, ("dp", "stream"), scatter_dimension=0, tiled=True),
        lax.psum_scatter(grad_gain_ffn, ("dp", "stream"), scatter_dimension=0, tiled=True),
        lax.psum_scatter(grad_shift_ffn, ("dp", "stream"), scatter_dimension=0, tiled=True),
        lax.psum_scatter(grad_w_visual, ("dp", "stream"), scatter_dimension=0, tiled=True),
        lax.psum_scatter(grad_b_visual, ("dp", "stream"), scatter_dimension=0, tiled=True),
    )
    return (
        out_text,
        out_visual,
        grad_text,
        grad_features,
        summed[0],
        summed[1],
        summed[2],
        summed[3],
        summed[4],
        summed[5],
        summed[6],
        summed[7],
        summed[8],
        summed[9],
        summed[10],
        summed[11],
        summed[12],
        summed[13],
        summed[14],
        summed[15],
        summed[16],
        grad_table_line,
        grad_table_x,
        grad_table_y,
    )


def solution(mesh):
    placed = (
        P("dp", "stream", None),
        P(("dp", "stream"), None, None),
        P("dp", None),
        P("dp", None),
        P(None, "dp", None),
        P(),
        P(),
        P(),
        P(),
        P(),
        P(),
        P(),
        P(),
        P(),
        P(),
        P(),
        P(),
        P(),
        P(),
        P(),
        P(),
        P(),
        P(),
        P(),
        P(),
        P("dp", "stream", None),
        P(("dp", "stream"), None, None),
    )
    return jax.shard_map(
        per_device,
        mesh=mesh,
        in_specs=placed,
        out_specs=(
            P("dp", "stream", None),
            P(("dp", "stream"), None, None),
            P("dp", "stream", None),
            P(("dp", "stream"), None, None),
            P(("dp", "stream"), None),
            P(("dp", "stream")),
            P(("dp", "stream"), None),
            P(("dp", "stream"), None),
            P(("dp", "stream")),
            P(("dp", "stream"), None),
            P(("dp", "stream")),
            P(("dp", "stream")),
            P(("dp", "stream")),
            P(("dp", "stream"), None),
            P(("dp", "stream")),
            P(("dp", "stream"), None),
            P(("dp", "stream")),
            P(("dp", "stream")),
            P(("dp", "stream")),
            P(("dp", "stream"), None),
            P(("dp", "stream")),
            P(),
            P(),
            P(),
        ),
        check_vma=False,
    )
```

profile of v0, /device:TPU:0, one launch (start us, length us, event | category | flops | bytes accessed | tf_op | source)
XLA Modules:
  0.0 2001.8 jit_solution(7847455535948680552)
XLA Ops:
  44.5 28.7 %all_gather.13 = bf16[8,49,768]{2,1,0:T(8,128)(2,1)S(1)} all-gather(bf16[2,49,768]{2,1,0:T(8,128)(2,1)S(1)} %reshape.777), channel_id=1, replica_groups=mesh['dp'=8,'stream'=4] {'stream'}, dimensions={0}, use_global_device_ids=true | all-gather | bytes 752640 | tf_op jit(solution)/shard_map/all_gather | solution.py:198
  73.1 28.4 %all_gather.15 = bf16[8,49,768]{2,1,0:T(8,128)(2,1)S(1)} all-gather(bf16[2,49,768]{2,1,0:T(8,128)(2,1)S(1)} %reshape.781), channel_id=1, replica_groups=mesh['dp'=8,'stream'=4] {'stream'}, dimensions={0}, use_global_device_ids=true | all-gather | bytes 752640 | tf_op jit(solution)/shard_map/all_gather | solution.py:197
  114.2 41.7 %all-gather.3.cloned.1.call-done = bf16[8,512,768]{2,1,0:T(8,128)(2,1)} async-done(((bf16[8,128,768]{2,1,0:T(8,128)(2,1)}), bf16[8,512,768]{2,1,0:T(8,128)(2,1)}) %all-gather.3.cloned.1.call-update) | async-done | bytes 6291472 | tf_op jit(solution)/shard_map/all_gather | solution.py:194
  172.3 98.9 %all-gather.5.cloned.1.call-done = bf16[8,512,768]{2,1,0:T(8,128)(2,1)} async-done(((bf16[8,128,768]{2,1,0:T(8,128)(2,1)}), bf16[8,512,768]{2,1,0:T(8,128)(2,1)}) %all-gather.5.cloned.1.call-update) | async-done | bytes 6291472 | tf_op jit(solution)/shard_map/all_gather | solution.py:193
  289.0 168.0 %while.34 = (s32[]{:T(128)}, bf16[2,4,128,12,64]{2,4,3,1,0:T(8,128)(2,1)}, f32[2,4,12,128,1]{3,2,1,4,0:T(8,128)S(1)}, bf16[2,4,561,12,64]{2,4,3,1,0:T(8,128)(2,1...) while((s32[]{:T(128)}, ...), condition=%wide.region_3.4_spmd.clone, body=%wide.region_0.3_spmd.clone.sunk | while | flops 1929044096 | bytes 169297600 | solution.py:222
  340.1 22.5 %fusion.417 = (f32[4,12,128]{2,1,0:T(8,128)S(1)}, f32[4,12,128,561]{2,3,1,0:T(8,128)}) fusion(f32[4,128,561,12]{1,3,2,0:T(8,128)} %fusion.412, f32[4,128,561,12]{1,3,2,0:T(8,128)} %fusion.413, f32[12,128,561]{1,2,0:T(8,128)S(1)} %copy.327, bf16[2,4,561,12,64]{2,4,3,1,0:T(8,128)(2,1)S(1)} %bitcast.372, s32[]{:T(128)S(6)} %copy.346, ...), kind=kOutput, calls=%fused_computation.447.clone.1 | convolution fusion | flops 461862912 | bytes 49886208 | tf_op jit(solution)/shard_map/while/body/eval_jaxpr/bqhd,bkhd->bhqk/dot_general | solution.py:70
  415.8 22.5 %fusion.417 = (f32[4,12,128]{2,1,0:T(8,128)S(1)}, f32[4,12,128,561]{2,3,1,0:T(8,128)}) fusion(f32[4,128,561,12]{1,3,2,0:T(8,128)} %fusion.412, f32[4,128,561,12]{1,3,2,0:T(8,128)} %fusion.413, f32[12,128,561]{1,2,0:T(8,128)S(1)} %copy.327, bf16[2,4,561,12,64]{2,4,3,1,0:T(8,128)(2,1)S(1)} %bitcast.372, s32[]{:T(128)S(6)} %copy.346, ...), kind=kOutput, calls=%fused_computation.447.clone.1 | convolution fusion | flops 461862912 | bytes 49886208 | tf_op jit(solution)/shard_map/while/body/eval_jaxpr/bqhd,bkhd->bhqk/dot_general | solution.py:70
  486.8 40.4 %multiply_convert_fusion.1 = (bf16[1122,3072]{1,0:T(8,128)(2,1)S(1)}, f32[1122,3072]{1,0:T(8,128)}, f32[1122,3072]{1,0:T(8,128)}) fusion(f32[3072]{0:T(1024)S(1)} %copy-done.95, bf16[768,3072]{1,0:T(8,128)(2,1)S(1)} %bitcast.413, f32[1122,768]{1,0:T(8,128)S(1)} %get-tuple-element.672, f32[768]{0:T(1024)S(1)} %copy-done.77, f32[768]{0:T(1024)S(1)} %copy-done.72, ...), kind=kOutput, calls=%fused_computation.224 | convolution fusion | flops 5526056448 | bytes 42660624 | tf_op jit(solution)/shard_map/dot_general | solution.py:250
  543.6 19.2 convert_reduce_fusion.1
  597.8 272.6 %while.35 = (s32[]{:T(128)}, bf16[2,4,128,12,64]{2,4,3,1,0:T(8,128)(2,1)}, f32[2,4,561,12,64]{2,4,3,1,0:T(8,128)}, f32[2,4,561,12,64]{2,4,3,1,0:T(8,128)}, f32[2...) while((s32[]{:T(128)}, ...), condition=%wide.region_17.18_spmd.clone, body=%wide.region_14.17_spmd.clone.sunk | while | flops 4240793088 | bytes 271616352 | solution.py:304
  618.5 14.5 fusion.434
  646.7 24.3 %multiply_reduce_fusion.7 = (f32[4,12,128]{2,1,0:T(8,128)S(1)}, f32[4,12,128,561]{2,3,1,0:T(8,128)S(1)}) fusion(f32[4,12,128,561]{2,3,1,0:T(8,128)} %fusion.431, f32[4,12,128]{2,1,0:T(8,128)S(1)} %dynamic-slice_bitcast_fusion.16, f32[4,128,561,12]{1,3,2,0:T(8,128)} %fusion.434, f32[4,128,561,12]{1,3,2,0:T(8,128)} %fusion.435, ...), kind=kOutput, calls=%fused_computation.111.clone.1 | convolution fusion | flops 468756480 | bytes 73057792 | tf_op jit(solution)/shard_map/while/body/eval_jaxpr/bqhd,bkhd->bhqk/dot_general | solution.py:70
  750.4 14.7 fusion.434
  778.7 24.3 %multiply_reduce_fusion.7 = (f32[4,12,128]{2,1,0:T(8,128)S(1)}, f32[4,12,128,561]{2,3,1,0:T(8,128)S(1)}) fusion(f32[4,12,128,561]{2,3,1,0:T(8,128)} %fusion.431, f32[4,12,128]{2,1,0:T(8,128)S(1)} %dynamic-slice_bitcast_fusion.16, f32[4,128,561,12]{1,3,2,0:T(8,128)} %fusion.434, f32[4,128,561,12]{1,3,2,0:T(8,128)} %fusion.435, ...), kind=kOutput, calls=%fused_computation.111.clone.1 | convolution fusion | flops 468756480 | bytes 73057792 | tf_op jit(solution)/shard_map/while/body/eval_jaxpr/bqhd,bkhd->bhqk/dot_general | solution.py:70
  1011.6 68.0 %reduce-scatter.36.cloned.1.call-done = bf16[128,6144]{1,0:T(8,128)(2,1)} async-done(((bf16[512,6144]{1,0:T(8,128)(2,1)}), bf16[128,6144]{1,0:T(8,128)(2,1)}) %reduce-scatter.36.cloned.1.call-update) | async-done | bytes 1572880
  1082.8 110.2 %reduce-scatter.34.cloned.1.call-done = bf16[128,6144]{1,0:T(8,128)(2,1)} async-done(((bf16[512,6144]{1,0:T(8,128)(2,1)}), bf16[128,6144]{1,0:T(8,128)(2,1)}) %reduce-scatter.34.cloned.1.call-update) | async-done | bytes 1572880
  1231.7 43.1 %all-reduce.10 = (f32[768]{0:T(1024)S(1)}, f32[768]{0:T(1024)S(1)}, f32[768]{0:T(1024)S(1)}, f32[768]{0:T(1024)S(1)}, f32[768]{0:T(1024)S(1)}, /*index=5*/f32[30...) all-reduce(f32[768]{0:T(1024)S(1)} %convert_reduce_fusion.2, ...), channel_id=7, replica_groups=mesh['dp'=8,'stream'=4] {'dp','stream'}, use_global_device_ids=true, to_apply=%region_25.26.clone | all-reduce | flops 11904 | bytes 95232
  1281.7 16.9 reduce-scatter.28.cloned.1.call-done
  1298.5 104.7 %reduce-scatter.22.cloned.1.call-done = f32[24,768]{1,0:T(8,128)} async-done(((f32[768,768]{1,0:T(8,128)}), f32[24,768]{1,0:T(8,128)}) %reduce-scatter.22.cloned.1.call-update) | async-done | bytes 73744 | tf_op jit(solution)/shard_map/reduce_scatter | solution.py:412
  1403.2 141.0 %reduce-scatter.30.cloned.1.call-done = f32[24,3072]{1,0:T(8,128)} async-done(((f32[768,3072]{1,0:T(8,128)}), f32[24,3072]{1,0:T(8,128)}) %reduce-scatter.30.cloned.1.call-update) | async-done | bytes 294928 | tf_op jit(solution)/shard_map/reduce_scatter | solution.py:421
  1544.2 142.1 %reduce-scatter.32.cloned.1.call-done = f32[96,768]{1,0:T(8,128)} async-done(((f32[3072,768]{1,0:T(8,128)}), f32[96,768]{1,0:T(8,128)}) %reduce-scatter.32.cloned.1.call-update) | async-done | bytes 294928 | tf_op jit(solution)/shard_map/reduce_scatter | solution.py:423
  1686.3 100.2 %reduce-scatter.38.cloned.1.call-done = f32[8,768]{1,0:T(8,128)} async-done(((f32[256,768]{1,0:T(8,128)}), f32[8,768]{1,0:T(8,128)}) %reduce-scatter.38.cloned.1.call-update) | async-done | bytes 24592
  1786.6 103.8 %reduce-scatter.26.cloned.1.call-done = f32[24,768]{1,0:T(8,128)} async-done(((f32[768,768]{1,0:T(8,128)}), f32[24,768]{1,0:T(8,128)}) %reduce-scatter.26.cloned.1.call-update) | async-done | bytes 73744 | tf_op jit(solution)/shard_map/reduce_scatter | solution.py:415
  1890.4 104.7 %reduce-scatter.24.cloned.1.call-done = f32[24,768]{1,0:T(8,128)} async-done(((f32[768,768]{1,0:T(8,128)}), f32[24,768]{1,0:T(8,128)}) %reduce-scatter.24.cloned.1.call-update) | async-done | bytes 73744 | tf_op jit(solution)/shard_map/reduce_scatter | solution.py:414
  (551 shorter events, 644.9 us)
Async XLA Ops:
  7.2 473.6 %copy-start = (bf16[768,768]{1,0:T(8,128)(2,1)S(1)}, bf16[768,768]{1,0:T(8,128)(2,1)}, u32[]{:S(2)}) copy-start(bf16[768,768]{1,0:T(8,128)(2,1)} %param.41) | copy-start | bytes 3538948
  7.2 148.8 %all-gather.3.cloned.1.call-start = ((), (), s32[]{:S(2)}) async-start(), calls=%async_computation.11 | async-start | bytes 7864320 | tf_op jit(solution)/shard_map/all_gather | solution.py:194
  15.8 255.4 %all-gather.5.cloned.1.call-start = ((), (), s32[]{:S(2)}) async-start(), calls=%async_computation.12 | async-start | bytes 7864320 | tf_op jit(solution)/shard_map/all_gather | solution.py:193
  21.8 987.2 %reduce-scatter.20.cloned.1.call-start = ((), (), s32[]{:S(2)}) async-start(), calls=%async_computation.14 | async-start | bytes 1966080 | tf_op jit(solution)/shard_map/reduce_scatter | solution.py:349
  40.5 61.0 %copy-start.51 = (s32[49,561]{1,0:T(8,128)}, s32[49,561]{1,0:T(8,128)S(1)}, u32[]{:S(2)}) copy-start(s32[49,561]{1,0:T(8,128)S(1)} %fusion.298) | copy-start | bytes 329872
  41.2 62.2 %copy-start.57 = (bf16[12,64]{1,0:T(8,128)(2,1)S(1)}, bf16[12,64]{1,0:T(8,128)(2,1)}, u32[]{:S(2)}) copy-start(bf16[12,64]{1,0:T(8,128)(2,1)} %param.55) | copy-start | bytes 4612
  43.0 64.9 %copy-start.55 = (bf16[12,64]{1,0:T(8,128)(2,1)S(1)}, bf16[12,64]{1,0:T(8,128)(2,1)}, u32[]{:S(2)}) copy-start(bf16[12,64]{1,0:T(8,128)(2,1)} %param.54) | copy-start | bytes 4612
  480.8 46.4 %slice-start.7 = ((s8[4718592]{0:T(1024)(128)(4,1)}), s8[4194304]{0:T(1024)(128)(4,1)S(1)}, s32[]{:S(2)}) async-start(s8[4718592]{0:T(1024)(128)(4,1)} %bitcast.410), calls=%async_computation.31 | async-start | bytes 8388608
  485.5 90.9 %copy-start.61 = (f32[1122]{0:T(1024)}, f32[1122]{0:T(1024)S(1)}, u32[]{:S(2)}) copy-start(f32[1122]{0:T(1024)S(1)} %broadcast_multiply_fusion.1) | copy-start | bytes 13468
  486.8 89.7 %copy-start.65 = (f32[1122]{0:T(1024)}, f32[1122]{0:T(1024)S(1)}, u32[]{:S(2)}) copy-start(f32[1122]{0:T(1024)S(1)} %fusion.310) | copy-start | bytes 13468
  597.7 272.6 %copy-start.26 = (pred[2,49,561]{2,1,0:T(8,128)(4,1)S(1)}, pred[2,49,561]{2,1,0:T(8,128)(4,1)}, u32[]{:S(2)}) copy-start(pred[2,49,561]{2,1,0:T(8,128)(4,1)} %broadcast_compare_fusion.2) | copy-start | bytes 164938
  897.5 112.9 %reduce-scatter.18.cloned.1.call-start = ((), (), s32[]{:S(2)}) async-start(), calls=%async_computation.13 | async-start | bytes 1966080 | tf_op jit(solution)/shard_map/reduce_scatter | solution.py:343
  910.0 169.6 %reduce-scatter.36.cloned.1.call-start = ((), (), s32[]{:S(2)}) async-start(), calls=%async_computation.22 | async-start | bytes 7864320
  932.7 260.4 %reduce-scatter.34.cloned.1.call-start = ((), (), s32[]{:S(2)}) async-start(), calls=%async_computation.21 | async-start | bytes 7864320
  955.4 343.2 %reduce-scatter.28.cloned.1.call-start = ((), (), s32[]{:S(2)}) async-start(), calls=%async_computation.18 | async-start | bytes 2433024 | tf_op jit(solution)/shard_map/reduce_scatter | solution.py:417
  960.7 442.6 %reduce-scatter.22.cloned.1.call-start = ((), (), s32[]{:S(2)}) async-start(), calls=%async_computation.15 | async-start | bytes 2433024 | tf_op jit(solution)/shard_map/reduce_scatter | solution.py:412
  977.6 566.6 %reduce-scatter.30.cloned.1.call-start = ((), (), s32[]{:S(2)}) async-start(), calls=%async_computation.19 | async-start | bytes 9732096 | tf_op jit(solution)/shard_map/reduce_scatter | solution.py:421
  990.3 696.0 %reduce-scatter.32.cloned.1.call-start = ((), (), s32[]{:S(2)}) async-start(), calls=%async_computation.20 | async-start | bytes 9732096 | tf_op jit(solution)/shard_map/reduce_scatter | solution.py:423
  1001.7 784.9 %reduce-scatter.38.cloned.1.call-start = ((), (), s32[]{:S(2)}) async-start(), calls=%async_computation.23 | async-start | bytes 811008
  1010.3 192.4 %copy-start.46 = (bf16[98,768]{1,0:T(8,128)(2,1)}, bf16[98,768]{1,0:T(8,128)(2,1)S(1)}, u32[]{:S(2)}) copy-start(bf16[98,768]{1,0:T(8,128)(2,1)S(1)} %reshape.797) | copy-start | bytes 451588
  1202.6 687.7 %reduce-scatter.26.cloned.1.call-start = ((), (), s32[]{:S(2)}) async-start(), calls=%async_computation.17 | async-start | bytes 2433024 | tf_op jit(solution)/shard_map/reduce_scatter | solution.py:415
  1207.8 787.3 %reduce-scatter.24.cloned.1.call-start = ((), (), s32[]{:S(2)}) async-start(), calls=%async_computation.16 | async-start | bytes 2433024 | tf_op jit(solution)/shard_map/reduce_scatter | solution.py:414
  1226.5 768.5 %copy-start.1 = (bf16[768,768]{1,0:T(8,128)(2,1)S(1)}, bf16[768,768]{1,0:T(8,128)(2,1)}, u32[]{:S(2)}) copy-start(bf16[768,768]{1,0:T(8,128)(2,1)} %param.41) | copy-start | bytes 3538948
  1229.4 50.7 %copy-start.35 = (bf16[256,768]{1,0:T(8,128)(2,1)S(1)}, bf16[256,768]{1,0:T(8,128)(2,1)}, u32[]{:S(2)}) copy-start(bf16[256,768]{1,0:T(8,128)(2,1)} %param.51) | copy-start | bytes 1179652
  (127 other events, 848.0 us)
Sparse Core Ops, SparseCore 0:
  15.9 139.9 all-gather.2
  157.5 113.6 all-gather.4
  897.6 33.6 reduce-scatter.19
  933.4 34.2 reduce-scatter.17
  969.9 109.7 reduce-scatter.35
  1081.8 111.2 reduce-scatter.33
  1198.9 99.5 reduce-scatter.27
  1305.2 97.9 reduce-scatter.21
  1409.7 134.4 reduce-scatter.29
  1551.6 134.7 reduce-scatter.31
  1692.0 94.4 reduce-scatter.37
  1792.3 98.0 reduce-scatter.25
  1897.1 97.9 reduce-scatter.23
where the time goes:
time: 2010 us; the launch traced here: 2000 us
  waiting for transfers between devices  1030 us (51%)
  matrix products  528 us (26%)
  local copies, waits for them, and re-layouts  173 us (9%)
  other arithmetic  125 us (6%)
  blocking collectives  100 us (5%)
  loops' own time  26.2 us (1%)
    unnamed x16, waiting for transfers between devices  279 us
    reduce_scatter x1, waiting for transfers between devices, per_device(): lax.psum_scatter(grad_w_down, ('dp', 'stream'), scatter_dimension=0, tile...  142 us
    reduce_scatter x1, waiting for transfers between devices, per_device(): lax.psum_scatter(grad_w_up, ('dp', 'stream'), scatter_dimension=0, tiled=...  141 us
    reduce_scatter x1, waiting for transfers between devices, per_device(): lax.psum_scatter(grad_w_query, ('dp', 'stream'), scatter_dimension=0, til...  105 us
    reduce_scatter x1, waiting for transfers between devices, per_device(): lax.psum_scatter(grad_w_key, ('dp', 'stream'), scatter_dimension=0, tiled...  105 us
    reduce_scatter x1, waiting for transfers between devices, per_device(): lax.psum_scatter(grad_w_value, ('dp', 'stream'), scatter_dimension=0, til...  104 us
    dot_general x5, matrix products, masked_scores(): jnp.einsum('bqhd,bkhd->bhqk', query, keys, preferred_element_type=jnp.flo...  100 us
    all_gather x1, waiting for transfers between devices, per_device(): lax.all_gather(text_part(key_all), 'stream', axis=1, tiled=True)  98.9 us
  transfers between devices with their start and end apart: 13, of which 11 were waited for; matrix products, arithmetic and copies ran while one was open for 11% of the time, Pallas kernels for 0%

commit v1 on v0

v1 whole, which is shorter than its diff:
```python
import math

import jax, jax.numpy as jnp
from jax import lax
from jax.experimental import pallas as pl
from jax.experimental.pallas import tpu as pltpu
from jax.sharding import PartitionSpec as P

HEADS = 12
RECEIPTS = 8
SPAN = 576
BINS = 160
NONE = -1e30


def thresholds(half, reach):
    exact = half // 2
    steps = half - exact
    return [
        int(math.floor(exact * (reach / exact) ** (power / steps) + 0.5))
        for power in range(1, steps)
    ]


def bucket(diff, count, reach):
    half = count // 2
    exact = half // 2
    dist = jnp.abs(diff)
    passed = jnp.where(diff > 0, half, 0)
    for limit in thresholds(half, reach):
        passed = passed + jnp.where(dist >= limit, 1, 0)
    return passed + jnp.minimum(dist, exact)


def dot(a, b, ca, cb):
    return lax.dot_general(a, b, (((ca,), (cb,)), ((), ())), preferred_element_type=jnp.float32)


def window(bounds_ref, receipt):
    base = pl.program_id(0) * 16
    first = bounds_ref[base + receipt]
    last = bounds_ref[base + receipt + 1]
    return first, last, (first // 16) * 16


def marks(receipt, first, rows, lanes, col_ref, row_ref, line_s, x_s, y_s):
    at_q = pl.multiple_of(jnp.minimum(first, SPAN - rows), 16)
    at_k = pl.multiple_of(jnp.minimum(first, SPAN - lanes), 16)
    col = col_ref[0, pl.ds(at_q, rows), :]
    row = pltpu.roll(row_ref[0], lax.rem(640 - at_k, 640), 1)[:, :lanes]
    mine = col[:, 3:4] == receipt
    shape = (rows, lanes)

    def gap(n):
        return jnp.broadcast_to(row[n : n + 1, :], shape) - jnp.broadcast_to(col[:, n : n + 1], shape)

    same = jnp.logical_and(
        jnp.broadcast_to(row[3:4, :], shape) == receipt,
        jnp.broadcast_to(col[:, 3:4], shape) == receipt,
    )
    line = jnp.where(same, bucket(gap(0), 32, 128), 32)
    across = bucket(gap(1), 64, 256)
    down = bucket(gap(2), 64, 256) + 64
    for c in range(lanes // 128):
        piece = slice(128 * c, 128 * (c + 1))
        line_s[c, :rows] = line[:, piece]
        x_s[c, :rows] = across[:, piece]
        y_s[c, :rows] = down[:, piece]
    return at_q, at_k, mine


def bias_of(pair, rows, lanes, plane_ref, lines_ref, line_s, x_s, y_s):
    halves = []
    for h in range(2):
        plane = jnp.broadcast_to(plane_ref[pl.ds(2 * pair + h, 1), :], (rows, 128))
        lines = jnp.broadcast_to(lines_ref[pl.ds(2 * pair + h, 1), :], (rows, 128))
        cols = []
        for c in range(lanes // 128):
            def look(table, index):
                return jnp.take_along_axis(table, index[c, :rows], axis=1, mode="promise_in_bounds")
            cols.append(look(plane, x_s) + look(plane, y_s) + look(lines, line_s))
        halves.append(cols[0] if len(cols) == 1 else jnp.concatenate(cols, axis=1))
    return jnp.concatenate(halves, axis=0)


def split_pair(value, scale=1.0):
    lane = lax.broadcasted_iota(jnp.int32, value.shape, 1)
    full = value.astype(jnp.float32) * scale
    low = jnp.where(lane < 64, full, 0.0).astype(value.dtype)
    high = jnp.where(lane < 64, 0.0, full).astype(value.dtype)
    return jnp.concatenate([low, high], axis=0)


def softmax(scores):
    expo = jnp.exp(scores - jnp.max(scores, axis=1, keepdims=True))
    return expo * (1.0 / jnp.sum(expo, axis=1, keepdims=True))


def by_size(bounds_ref, run):
    def step(receipt, carry):
        first, last, start = window(bounds_ref, receipt)
        span = last - start
        for low, rows, lanes in ((0, 64, 128), (64, 128, 128), (128, 192, 256)):
            inside = span > low
            if rows < 192:
                inside = jnp.logical_and(inside, span <= rows)

            @pl.when(inside)
            def _(rows=rows, lanes=lanes):
                run(receipt, first, last, start, rows, lanes)

        return carry

    lax.fori_loop(0, RECEIPTS, step, 0)


def forward_kernel(bounds_ref, q_ref, k_ref, v_ref, col_ref, row_ref, plane_ref, lines_ref, out_ref, line_s, x_s, y_s):
    out_ref[...] = jnp.zeros_like(out_ref)

    def run(receipt, first, last, start, rows, lanes):
        at_q, at_k, mine = marks(receipt, start, rows, lanes, col_ref, row_ref, line_s, x_s, y_s)

        def pair_step(pair, carry):
            at = pl.multiple_of(pair * 128, 128)
            q = split_pair(q_ref[0, pl.ds(at_q, rows), pl.ds(at, 128)], 0.125)
            k = k_ref[0, pl.ds(at_k, lanes), pl.ds(at, 128)]
            v = split_pair(v_ref[0, pl.ds(at_k, lanes), pl.ds(at, 128)])
            scores = dot(q, k, 1, 1) + bias_of(pair, rows, lanes, plane_ref, lines_ref, line_s, x_s, y_s)
            shares = softmax(scores).astype(jnp.bfloat16)
            shares = jnp.concatenate([shares[:rows], shares[rows:]], axis=1)
            context = dot(shares, v, 1, 0)
            here = (0, pl.ds(at_q, rows), pl.ds(at, 128))
            out_ref[here] = jnp.where(mine, context, out_ref[here].astype(jnp.float32)).astype(jnp.bfloat16)
            return carry

        lax.fori_loop(0, HEADS // 2, pair_step, 0)

    by_size(bounds_ref, run)


def backward_kernel(
    bounds_ref, q_ref, k_ref, v_ref, g_ref, col_ref, row_ref, plane_ref, lines_ref,
    dq_ref, dk_ref, dv_ref, bins_ref, line_s, x_s, y_s, ds_s,
):
    dq_ref[...] = jnp.zeros_like(dq_ref)
    dk_ref[...] = jnp.zeros_like(dk_ref)
    dv_ref[...] = jnp.zeros_like(dv_ref)

    @pl.when(pl.program_id(0) == 0)
    def _():
        bins_ref[...] = jnp.zeros_like(bins_ref)
        ds_s[...] = jnp.zeros_like(ds_s)

    def run(receipt, first, last, start, rows, lanes):
        at_q, at_k, mine = marks(receipt, start, rows, lanes, col_ref, row_ref, line_s, x_s, y_s)
        mine_k = col_ref[0, pl.ds(at_k, lanes), :][:, 3:4] == receipt

        def pair_step(pair, carry):
            at = pl.multiple_of(pair * 128, 128)
            rows_at = (0, pl.ds(at_q, rows), pl.ds(at, 128))
            keys_at = (0, pl.ds(at_k, lanes), pl.ds(at, 128))
            q = split_pair(q_ref[rows_at], 0.125)
            k = k_ref[keys_at]
            v = v_ref[keys_at]
            g = jnp.where(mine, g_ref[rows_at].astype(jnp.float32), 0.0).astype(jnp.bfloat16)
            g = split_pair(g)
            scores = dot(q, k, 1, 1) + bias_of(pair, rows, lanes, plane_ref, lines_ref, line_s, x_s, y_s)
            probs = softmax(scores)
            shares = probs.astype(jnp.bfloat16)
            gp = dot(g, v, 1, 1)
            inner = jnp.sum(probs * gp, axis=1, keepdims=True)
            gs = (probs * (gp - inner)).astype(jnp.bfloat16)
            wide = gs.astype(jnp.float32)
            for h in range(2):
                for c in range(0, lanes, 128):
                    ds_s[c // 128, pl.ds(2 * pair + h, rows, stride=16), :] = wide[h * rows : (h + 1) * rows, c : c + 128]
            dv = dot(shares, g, 0, 0)
            dk = dot(gs, q, 0, 0)
            dq = dot(jnp.concatenate([gs[:rows], gs[rows:]], axis=1), split_pair(k, 0.125), 1, 0)

            def put(ref, where, mask, value):
                ref[where] = jnp.where(mask, value, ref[where].astype(jnp.float32)).astype(jnp.bfloat16)

            put(dq_ref, rows_at, mine, dq)
            put(dk_ref, keys_at, mine_k, dk)
            put(dv_ref, keys_at, mine_k, dv)
            return carry

        lax.fori_loop(0, HEADS // 2, pair_step, 0)
        group = 2
        level = lax.broadcasted_iota(jnp.int32, (BINS, 128), 0)

        def bin_step(step, total):
            hots, terms = [], []
            for n in range(group):
                i = step * group + n
                for c in range(lanes // 128):
                    def spread(s, count):
                        return jnp.broadcast_to(s[c, pl.ds(i, 1), :], (count, 128))
                    index = jnp.concatenate([spread(x_s, 64), spread(y_s, 64), spread(line_s, 32) + 128], axis=0)
                    hots.append(jnp.where(level == index, 1.0, 0.0).astype(jnp.bfloat16))
                    terms.append(ds_s[c, pl.ds(pl.multiple_of(i * 16, 16), 16), :].astype(jnp.bfloat16))
            return total + dot(jnp.concatenate(hots, axis=1), jnp.concatenate(terms, axis=1), 1, 1)

        total = lax.fori_loop(
            (first - at_q) // group, pl.cdiv(last - at_q, group), bin_step, jnp.zeros((BINS, 16), jnp.float32)
        )
        bins_ref[:, :16] += total

    by_size(bounds_ref, run)


def attend(bounds, q, k, v, col, row, plane, lines):
    rows, span, width = q.shape
    wide = pl.BlockSpec((1, span, width), lambda i, *_: (i, 0, 0))
    spec = pltpu.PrefetchScalarGridSpec(
        num_scalar_prefetch=1,
        grid=(rows,),
        in_specs=[wide, wide, wide,
            pl.BlockSpec((1, span, 128), lambda i, *_: (i, 0, 0)),
            pl.BlockSpec((1, 8, 640), lambda i, *_: (i, 0, 0)),
            pl.BlockSpec((HEADS, 128), lambda i, *_: (0, 0)),
            pl.BlockSpec((HEADS, 128), lambda i, *_: (0, 0)),
        ],
        out_specs=wide,
        scratch_shapes=[pltpu.VMEM((2, 192, 128), jnp.int32)] * 3,
    )
    return pl.pallas_call(
        forward_kernel,
        grid_spec=spec,
        out_shape=jax.ShapeDtypeStruct(q.shape, q.dtype),
        compiler_params=pltpu.CompilerParams(vmem_limit_bytes=40 * 1024 * 1024),
        name="attend",
    )(bounds, q, k, v, col, row, plane, lines)


def attend_back(bounds, q, k, v, g, col, row, plane, lines):
    rows, span, width = q.shape
    wide = pl.BlockSpec((1, span, width), lambda i, *_: (i, 0, 0))
    spec = pltpu.PrefetchScalarGridSpec(
        num_scalar_prefetch=1,
        grid=(rows,),
        in_specs=[wide, wide, wide, wide,
            pl.BlockSpec((1, span, 128), lambda i, *_: (i, 0, 0)),
            pl.BlockSpec((1, 8, 640), lambda i, *_: (i, 0, 0)),
            pl.BlockSpec((HEADS, 128), lambda i, *_: (0, 0)),
            pl.BlockSpec((HEADS, 128), lambda i, *_: (0, 0)),
        ],
        out_specs=[wide, wide, wide, pl.BlockSpec((BINS, 128), lambda i, *_: (0, 0))],
        scratch_shapes=[pltpu.VMEM((2, 192, 128), jnp.int32)] * 3 + [pltpu.VMEM((2, 192 * 16, 128), jnp.float32)],
    )
    same = jax.ShapeDtypeStruct(q.shape, q.dtype)
    return pl.pallas_call(
        backward_kernel,
        grid_spec=spec,
        out_shape=[same, same, same, jax.ShapeDtypeStruct((BINS, 128), jnp.float32)],
        compiler_params=pltpu.CompilerParams(vmem_limit_bytes=48 * 1024 * 1024),
        name="attend_back",
    )(bounds, q, k, v, g, col, row, plane, lines)


DP = "dp"
STREAM = "stream"


def layer_norm(values, gain, shift):
    centred = values - jnp.mean(values, axis=-1, keepdims=True)
    spread = jnp.mean(centred * centred, axis=-1, keepdims=True)
    return centred * lax.rsqrt(spread + 1e-05) * gain + shift


def gelu_exact(values):
    return jax.nn.gelu(values, approximate=False)


def swap(value, axis, bit):
    count = lax.axis_size(axis)
    return lax.ppermute(value, axis, [(i, i ^ bit) for i in range(count)])


def bits_of(axis):
    count = lax.axis_size(axis)
    return [1 << n for n in range(count.bit_length() - 1)]


def stages(flip):
    core, *chips = bits_of(DP)
    if flip:
        chips = chips[::-1]
    return [(DP, core)] + [(DP, bit) for bit in chips] + [(STREAM, bit) for bit in bits_of(STREAM)]


def scatter_sum(value, flip):
    names = [(axis, bit) for axis in (DP, STREAM) for bit in bits_of(axis)[::-1]]
    value = value.reshape((2,) * len(names) + value.shape[1:])
    for stage in stages(flip):
        axis, bit = stage
        dim = names.index(stage)
        side = (lax.axis_index(axis) // bit) % 2
        given = lax.dynamic_index_in_dim(value, 1 - side, dim, keepdims=False)
        kept = lax.dynamic_index_in_dim(value, side, dim, keepdims=False)
        value = kept.astype(jnp.float32) + swap(given.astype(jnp.bfloat16), axis, bit).astype(jnp.float32)
        names.pop(dim)
    return value


def sum_all(value):
    for axis, bit in stages(False):
        value = value + swap(value, axis, bit)
    return value


def by_rows(value):
    count = lax.axis_size(STREAM)
    place = lax.axis_index(STREAM)
    block = value.shape[0] // count
    parts = [lax.dynamic_slice_in_dim(value, place * block, block, 0)]
    for shift in range(1, count):
        sent = lax.dynamic_slice_in_dim(value, (place + shift) % count * block, block, 0)
        parts.append(lax.ppermute(sent, STREAM, [(i, (i + shift) % count) for i in range(count)]))
    stacked = jnp.stack(parts)
    order = (place - jnp.arange(count)) % count
    ordered = [lax.dynamic_index_in_dim(stacked, order[n], 0, keepdims=False) for n in range(count)]
    return jnp.concatenate(ordered, axis=1)


def by_slots(value):
    return lax.all_to_all(value, STREAM, 1, 0, tiled=True)


def per_device(
    text_input,
    visual_features,
    receipt_text,
    receipt_visual,
    boxes,
    w_query,
    b_query,
    w_key,
    w_value,
    b_value,
    w_out,
    b_out,
    gain_attn,
    shift_attn,
    w_up,
    b_up,
    w_down,
    b_down,
    gain_ffn,
    shift_ffn,
    w_visual,
    b_visual,
    table_line,
    table_x,
    table_y,
    cotangent_text,
    cotangent_visual,
):
    floating = jnp.float32
    narrow = jnp.bfloat16
    width = text_input.shape[-1]
    rows, visual, channels = visual_features.shape
    text = receipt_text.shape[1]
    slots = text + visual
    world = lax.axis_size(DP) * lax.axis_size(STREAM)
    place = lax.axis_index(STREAM)
    first_row = place * rows

    text_rows = lax.all_to_all(text_input, STREAM, 0, 1, tiled=True)
    kept = lax.optimization_barrier((text_rows, cotangent_text))
    text_rows = kept[0]
    cotangent_rows = lax.all_to_all(kept[1], STREAM, 0, 1, tiled=True)

    def pad(value, fill=0):
        extra = SPAN - value.shape[1]
        return jnp.pad(value, ((0, 0), (0, extra)) + ((0, 0),) * (value.ndim - 2), constant_values=fill)

    seg_text = lax.dynamic_slice_in_dim(receipt_text, first_row, rows, 0)
    seg_visual = lax.dynamic_slice_in_dim(receipt_visual, first_row, rows, 0)
    box = lax.dynamic_slice_in_dim(boxes, first_row, rows, 1)
    seg = pad(jnp.concatenate([seg_text, seg_visual], axis=1), RECEIPTS)
    index = jnp.arange(SPAN, dtype=jnp.int32)
    ahead = (seg[:, None, :] < seg[:, :, None]) | (
        (seg[:, None, :] == seg[:, :, None]) & (index[None, :] < index[:, None])[None]
    )
    target = jnp.sum(ahead.astype(jnp.int32), axis=2)
    moved = target[:, None, :] == index[None, :, None]
    position = jnp.where(index < text, index, index - text)
    facts = jnp.stack(
        [jnp.broadcast_to(position, seg.shape), pad(box[0]), pad(box[1]), seg], axis=1
    )
    facts = jnp.sum(jnp.where(moved[:, None], facts[:, :, None, :], 0), axis=3)
    col = jnp.pad(jnp.swapaxes(facts, 1, 2), ((0, 0), (0, 0), (0, 124)))
    row = jnp.pad(facts, ((0, 0), (0, 4), (0, 640 - SPAN)), constant_values=RECEIPTS)
    bounds = jnp.sum(
        (seg[:, None, :] < jnp.arange(16, dtype=jnp.int32)[None, :, None]).astype(jnp.int32), axis=2
    ).reshape(-1)
    plane = jnp.concatenate([table_x, table_y], axis=1).astype(floating)
    lines = jnp.pad(table_line.astype(floating), ((0, 0), (0, 96)), constant_values=NONE)

    moving = moved.astype(narrow)

    def sort(value):
        return jnp.einsum("rps,rsd->rpd", moving[:, :, : value.shape[1]], value, preferred_element_type=floating)

    def unsort(value):
        return jnp.einsum("rps,rpd->rsd", moving, value, preferred_element_type=floating)

    features = jnp.einsum(
        "rpv,rvc->rpc", moving[:, :, text:slots], visual_features, preferred_element_type=floating
    ).astype(narrow)
    is_visual = jnp.sum(moving[:, :, text:slots].astype(floating), axis=2)[:, :, None]
    features_flat = features.reshape(-1, channels)
    visual_pre = jnp.einsum("rpc,cd->rpd", features, w_visual, preferred_element_type=floating)
    visual_pre = (visual_pre + b_visual.astype(floating)) * is_visual
    stream_in = (sort(text_rows) + visual_pre).reshape(-1, width)
    entered = stream_in.astype(narrow)
    query = (
        jnp.dot(entered, w_query, preferred_element_type=floating) + b_query.astype(floating)
    ).astype(narrow)
    key = jnp.dot(entered, w_key, preferred_element_type=floating).astype(narrow)
    value = (
        jnp.dot(entered, w_value, preferred_element_type=floating) + b_value.astype(floating)
    ).astype(narrow)

    def rowwise(array):
        return array.reshape(rows, SPAN, width)

    context = attend(bounds, rowwise(query), rowwise(key), rowwise(value), col, row, plane, lines)
    context = context.reshape(-1, width)
    grad_outcome = sort(jnp.concatenate([cotangent_rows, cotangent_visual], axis=1)).reshape(-1, width)

    attended = jnp.dot(context, w_out, preferred_element_type=floating) + b_out.astype(floating)
    norm_one, back_one = jax.vjp(
        layer_norm, stream_in + attended, gain_attn.astype(floating), shift_attn.astype(floating)
    )
    hidden = norm_one.astype(narrow)
    inner_up = jnp.dot(hidden, w_up, preferred_element_type=floating) + b_up.astype(floating)
    active, back_gelu = jax.vjp(gelu_exact, inner_up)
    active_low = active.astype(narrow)
    branch = jnp.dot(active_low, w_down, preferred_element_type=floating) + b_down.astype(floating)
    outcome, back_two = jax.vjp(
        layer_norm, norm_one + branch, gain_ffn.astype(floating), shift_ffn.astype(floating)
    )
    out_rows = unsort(rowwise(outcome.astype(narrow))).astype(narrow)
    out_text = by_slots(out_rows[:, :text])
    out_visual = out_rows[:, text:slots]

    grad_top, grad_gain_ffn, grad_shift_ffn = back_two(grad_outcome)
    grad_branch = grad_top.astype(narrow)
    grad_b_down = jnp.sum(grad_branch, axis=0, dtype=floating)
    grad_w_down = jnp.einsum("tf,td->fd", active_low, grad_branch, preferred_element_type=floating)
    down_sum = scatter_sum(grad_w_down.reshape(world, -1, width), False)
    grad_active = jnp.einsum("td,fd->tf", grad_branch, w_down, preferred_element_type=floating)
    grad_inner = back_gelu(grad_active)[0].astype(narrow)
    grad_b_up = jnp.sum(grad_inner, axis=0, dtype=floating)
    grad_w_up = jnp.einsum("td,tf->df", hidden, grad_inner, preferred_element_type=floating)
    up_sum = scatter_sum(grad_w_up.reshape(world, -1, w_up.shape[1]), True)
    grad_norm = grad_top + jnp.einsum("tf,df->td", grad_inner, w_up, preferred_element_type=floating)
    grad_mid, grad_gain_attn, grad_shift_attn = back_one(grad_norm)
    grad_attended = grad_mid.astype(narrow)
    grad_b_out = jnp.sum(grad_attended, axis=0, dtype=floating)
    grad_w_out = jnp.einsum("td,te->de", context, grad_attended, preferred_element_type=floating)
    out_sum = scatter_sum(grad_w_out.reshape(world, -1, width), False)
    grad_context = jnp.einsum("te,de->td", grad_attended, w_out, preferred_element_type=floating).astype(narrow)

    grad_query, grad_key, grad_value, bins = attend_back(
        bounds, rowwise(query), rowwise(key), rowwise(value), rowwise(grad_context), col, row, plane, lines
    )
    grad_query, grad_key, grad_value = (part.reshape(-1, width) for part in (grad_query, grad_key, grad_value))
    grad_stream = grad_mid + jnp.einsum("te,de->td", grad_query, w_query, preferred_element_type=floating)
    grad_stream = grad_stream + jnp.einsum("te,de->td", grad_key, w_key, preferred_element_type=floating)
    grad_stream = grad_stream + jnp.einsum("te,de->td", grad_value, w_value, preferred_element_type=floating)
    grad_low = grad_stream.astype(narrow)
    back_rows = unsort(rowwise(grad_low)).astype(narrow)
    grad_text = by_slots(back_rows[:, :text]).astype(floating)
    grad_visual = back_rows[:, text:slots]
    grad_w_query = jnp.einsum("td,te->de", entered, grad_query, preferred_element_type=floating)
    grad_b_query = jnp.sum(grad_query, axis=0, dtype=floating)
    grad_w_key = jnp.einsum("td,te->de", entered, grad_key, preferred_element_type=floating)
    grad_w_value = jnp.einsum("td,te->de", entered, grad_value, preferred_element_type=floating)
    grad_b_value = jnp.sum(grad_value, axis=0, dtype=floating)
    grad_w_visual = jnp.einsum("rvc,rvd->cd", visual_features, grad_visual, preferred_element_type=floating)
    grad_b_visual = jnp.sum(grad_visual, axis=(0, 1), dtype=floating)
    grad_features = jnp.einsum("rvd,cd->rvc", grad_visual, w_visual, preferred_element_type=floating)
    first = scatter_sum(
        jnp.concatenate([part.reshape(world, -1, width) for part in (grad_w_query, grad_w_visual)], axis=1), False
    )
    second = scatter_sum(
        jnp.concatenate([part.reshape(world, -1, width) for part in (grad_w_key, grad_w_value)], axis=1), True
    )
    step = width // world
    small = sum_all(
        jnp.concatenate(
            [
                jnp.stack(
                    [
                        grad_b_query, grad_b_value, grad_b_out, grad_gain_attn, grad_shift_attn,
                        grad_b_down, grad_gain_ffn, grad_shift_ffn, grad_b_visual,
                    ]
                ),
                grad_b_up.reshape(-1, width),
                jnp.pad(bins.reshape(-1), (0, -bins.size % width)).reshape(-1, width),
            ],
            axis=0,
        )
    )
    device = lax.axis_index(DP) * lax.axis_size(STREAM) + place
    mine = lax.dynamic_slice_in_dim(small[:9], device * step, step, 1)
    up_step = w_up.shape[1] // world
    ups = small[9 : 9 + w_up.shape[1] // width].reshape(-1)
    bins = small[9 + w_up.shape[1] // width :].reshape(-1)[: bins.size].reshape(bins.shape)[:, :HEADS].T
    return (
        out_text,
        out_visual,
        grad_text,
        grad_features,
        first[:step],
        mine[0],
        second[:step],
        second[step:],
        mine[1],
        out_sum,
        mine[2],
        mine[3],
        mine[4],
        up_sum,
        lax.dynamic_slice_in_dim(ups, device * up_step, up_step, 0),
        down_sum,
        mine[5],
        mine[6],
        mine[7],
        first[step:],
        mine[8],
        bins[:, 128:160],
        bins[:, :64],
        bins[:, 64:128],
    )


def solution(mesh):
    placed = (
        P("dp", "stream", None),
        P(("dp", "stream"), None, None),
        P("dp", None),
        P("dp", None),
        P(None, "dp", None),
        P(),
        P(),
        P(),
        P(),
        P(),
        P(),
        P(),
        P(),
        P(),
        P(),
        P(),
        P(),
        P(),
        P(),
        P(),
        P(),
        P(),
        P(),
        P(),
        P(),
        P("dp", "stream", None),
        P(("dp", "stream"), None, None),
    )
    return jax.shard_map(
        per_device,
        mesh=mesh,
        in_specs=placed,
        out_specs=(
            P("dp", "stream", None),
            P(("dp", "stream"), None, None),
            P("dp", "stream", None),
            P(("dp", "stream"), None, None),
            P(("dp", "stream"), None),
            P(("dp", "stream")),
            P(("dp", "stream"), None),
            P(("dp", "stream"), None),
            P(("dp", "stream")),
            P(("dp", "stream"), None),
            P(("dp", "stream")),
            P(("dp", "stream")),
            P(("dp", "stream")),
            P(("dp", "stream"), None),
            P(("dp", "stream")),
            P(("dp", "stream"), None),
            P(("dp", "stream")),
            P(("dp", "stream")),
            P(("dp", "stream")),
            P(("dp", "stream"), None),
            P(("dp", "stream")),
            P(),
            P(),
            P(),
        ),
        check_vma=False,
    )
```

time: 2010 us -> 696 us (0.35)
  waiting for transfers between devices: 1030 us -> 99.7 us
  matrix products: 528 us -> 147 us
  Pallas kernels: 0 us -> 257 us
  local copies, waits for them, and re-layouts: 173 us -> 71.4 us
  blocking collectives: 100 us -> 0 us
  other arithmetic: 125 us -> 45.4 us
  starting transfers between devices: 1.33 us -> 67.2 us
  loops' own time: 26.2 us -> 0 us
    reduce_scatter x8 -> x0, waiting for transfers between devices: 613 us -> none  [the longest x1 142 us: per_device(): lax.psum_scatter(grad_w_down, ('dp', 'stream'), scatter_dimension=0, tile...]
    dot_general x47 -> x7, matrix products: 390 us -> 18.3 us  [the longest x2 6.67 us: sort(): jnp.einsum('rps,rsd->rpd', moving[:, :, :value.shape[1]], value, preferre...]
    unnamed x16 -> x0, waiting for transfers between devices: 279 us -> none
    pallas_call x0 -> x2, Pallas kernels: none -> 257 us  [the longest x1 182 us: attend_back(): pl.pallas_call(backward_kernel, grid_spec=spec, out_shape=[same, same, sa...]
    all_gather x2 -> x0, waiting for transfers between devices: 141 us -> none  [the longest x1 98.9 us: per_device(): lax.all_gather(text_part(key_all), 'stream', axis=1, tiled=True)]
    ppermute x0 -> x30, waiting for transfers between devices: none -> 71.5 us  [swap(): return lax.ppermute(value, axis, [(i, i ^ bit) for i in range(count)])]
    all_gather x2 -> x0, blocking collectives: 57.1 us -> none  [the longest x1 28.7 us: per_device(): lax.all_gather(visual_part(value_all), 'stream', axis=0, tiled=True)]
    unnamed x241 -> x220, local copies, waits for them, and re-layouts: 66.7 us -> 20.1 us
  transfers between devices with their start and end apart: 13 -> 34, of which waited for: 11 -> 20; matrix products, arithmetic and copies ran while one was open for 11% -> 24% of each run, Pallas kernels for 0% -> 11%
where the time goes in v1:
time: 696 us; the launch traced here: 690 us
  Pallas kernels  257 us (37%)
  matrix products  147 us (21%)
  waiting for transfers between devices  99.7 us (14%)
  local copies, waits for them, and re-layouts  71.4 us (10%)
  starting transfers between devices  67.2 us (10%)
  other arithmetic  45.4 us (7%)
    pallas_call x1, Pallas kernels, attend_back(): pl.pallas_call(backward_kernel, grid_spec=spec, out_shape=[same, same, sa...  182 us
    pallas_call x1, Pallas kernels, attend(): pl.pallas_call(forward_kernel, grid_spec=spec, out_shape=jax.ShapeDtypeSt...  74.3 us
    ppermute x30, waiting for transfers between devices, swap(): return lax.ppermute(value, axis, [(i, i ^ bit) for i in range(count)])  71.5 us
    dot_general x1, matrix products, per_device(): jnp.dot(hidden, w_up, preferred_element_type=floating)  42.5 us
    all_to_all x2, starting transfers between devices, by_slots(): return lax.all_to_all(value, STREAM, 1, 0, tiled=True)  33.4 us
    ppermute x30, starting transfers between devices, swap(): return lax.ppermute(value, axis, [(i, i ^ bit) for i in range(count)])  22.5 us
    all_to_all x1, waiting for transfers between devices, per_device(): text_rows = lax.all_to_all(text_input, STREAM, 0, 1, tiled=True)  20.3 us
    unnamed x220, local copies, waits for them, and re-layouts  20.1 us
  transfers between devices with their start and end apart: 34, of which 20 were waited for; matrix products, arithmetic and copies ran while one was open for 24% of the time, Pallas kernels for 11%

profile of v1, /device:TPU:0, one launch (start us, length us, event | category | flops | bytes accessed | tf_op | source)
XLA Modules:
  0.0 690.3 jit_solution(10931725611671399107)
XLA Ops:
  0.8 6.5 all-to-all-start
  23.9 20.3 %all-to-all-done = bf16[8,128,768]{2,1,0:T(8,128)(2,1)S(1)} async-done(((bf16[8,128,768]{2,1,0:T(8,128)(2,1)}), bf16[8,128,768]{2,1,0:T(8,128)(2,1)S(1)}, u32[]{:S(2)}, u32[]{:S(2)}) %all-to-all-start) | async-done | bytes 1572896 | tf_op jit(solution)/shard_map/all_to_all | solution.py:370
  45.5 4.9 all-to-all-start.2
  50.4 4.5 fusion.17
  54.9 4.7 multiply_add_fusion.1
  67.4 74.3 %attend.1 = bf16[2,576,768]{2,1,0:T(8,128)(2,1)S(1)} custom-call(s32[32]{0:T(128)S(1)} %copy-done.9, bf16[2,576,768]{2,1,0:T(8,128)(2,1)S(1)} %bitcast.243, bf16[2,576,768]{2,1,0:T(8,128)(2,1)S(1)} %bitcast.241, bf16[2,576,768]{2,1,0:T(8,128)(2,1)S(1)} %bitcast.245, s32[2,576,128]{2,1,0:T(8,128)S(1)} %pad.29.col_ref, s32[2,8,640]{2,1,0:T(8,128)S(1)} %copy-done.5, ...), custom_call_target="tpu_custom_call" | custom-call | tf_op jit(solution)/shard_map/attend/pallas_call | solution.py:228
  152.6 42.5 %multiply_convert_fusion = (bf16[1152,3072]{1,0:T(8,128)(2,1)S(1)}, f32[1152,3072]{1,0:T(8,128)}, f32[1152,3072]{1,0:T(8,128)}) fusion(f32[3072]{0:T(1024)} %convert_element_type.367, bf16[768,3072]{1,0:T(8,128)(2,1)} %param.41, f32[1152,768]{1,0:T(8,128)} %copy-done.18, f32[768]{0:T(1024)} %convert_element_type.365, f32[768]{0:T(1024)} %convert_element_type.364, ...), kind=kOutput, calls=%fused_computation.4 | convolution fusion | flops 5673811968 | bytes 43674624 | tf_op jit(solution)/shard_map/dot_general | solution.py:439
  195.1 11.3 %fusion.80 = (f32[1152]{0:T(1024)S(1)}, f32[1152,768]{1,0:T(8,128)S(1)}) fusion(f32[768]{0:T(1024)S(1)} %copy-done.74, bf16[1152,3072]{1,0:T(8,128)(2,1)S(1)} %get-tuple-element.145, bf16[3072,768]{1,0:T(8,128)(2,1)} %param.43, f32[768]{0:T(1024)S(1)} %copy-done.72, f32[768]{0:T(1024)S(1)} %copy-done.61, f32[1152]{0:T(1024)S(1)} %copy-done.54, ...), kind=kOutput, calls=%fused_computation.218 | convolution fusion | flops 5442010112 | bytes 18897408 | tf_op jit(solution)/shard_map/dot_general | solution.py:442
  220.3 19.5 %convert_reduce_fusion = (f32[3072]{0:T(1024)}, bf16[1152,3072]{1,0:T(8,128)(2,1)}) fusion(f32[1152,3072]{1,0:T(8,128)} %get-tuple-element.146, f32[1152,3072]{1,0:T(8,128)} %get-tuple-element.167, bf16[1152,768]{1,0:T(8,128)(2,1)S(1)} %get-tuple-element.138, bf16[3072,768]{1,0:T(8,128)(2,1)} %param.43), kind=kOutput, calls=%fused_computation.2 | convolution fusion | flops 5492438016 | bytes 41889792 | tf_op jit(solution)/shard_map/td,fd->tf/dot_general | solution.py:455
  239.8 14.1 %multiply_reduce_fusion = (f32[768]{0:T(1024)}, f32[1152]{0:T(1024)S(1)}, f32[768]{0:T(1024)}, f32[1152,768]{1,0:T(8,128)S(1)}) fusion(f32[1152,768]{1,0:T(8,128)} %copy-done.18, f32[1152]{0:T(1024)} %fusion.65, f32[1152]{0:T(1024)} %copy-done.48, f32[768]{0:T(1024)} %convert_element_type.364, bf16[1152,3072]{1,0:T(8,128)(2,1)} %get-tuple-element.174, ...), kind=kOutput, calls=%fused_computation.44 | convolution fusion | flops 5444662272 | bytes 22440960 | tf_op jit(solution)/shard_map/tf,df->td/dot_general | solution.py:460
  259.1 182.5 %attend_back.1 = (bf16[2,576,768]{2,1,0:T(8,128)(2,1)S(1)}, bf16[2,576,768]{2,1,0:T(8,128)(2,1)S(1)}, bf16[2,576,768]{2,1,0:T(8,128)(2,1)S(1)}, f32[160,128]{1,0:T(8,128)S(1)}) custom-call(s32[32]{0:T(128)S(1)} %copy-done.10, bf16[2,576,768]{2,1,0:T(8,128)(2,1)} %bitcast.244, bf16[2,576,768]{2,1,0:T(8,128)(2,1)} %bitcast.242, ...), custom_call_target="tpu_custom_call" | custom-call | tf_op jit(solution)/shard_map/attend_back/pallas_call | solution.py:253
  451.7 9.7 %fusion.71 = f32[768,3072]{1,0:T(8,128)} fusion(bf16[1152,3072]{1,0:T(8,128)(2,1)S(1)} %bitcast.289, f32[1152,768]{1,0:T(8,128)S(1)} %copy-done.20, f32[768]{0:T(1024)S(1)} %copy-done.73, f32[768]{0:T(1024)S(1)} %copy-done.62, f32[1152]{0:T(1024)S(1)} %copy-done.55, f32[1152]{0:T(1024)S(1)} %copy-done.50), kind=kOutput, calls=%fused_computation.212 | convolution fusion | flops 5440241664 | bytes 20069376 | tf_op jit(solution)/shard_map/td,tf->df/dot_general | solution.py:458
  461.5 9.0 %fusion.85 = f32[3072,768]{1,0:T(8,128)} fusion(bf16[1152,3072]{1,0:T(8,128)(2,1)S(1)} %bitcast.291, bf16[1152,768]{1,0:T(8,128)(2,1)S(1)} %copy-done.40), kind=kOutput, calls=%fused_computation.223 | convolution fusion | flops 5435817984 | bytes 18284544 | tf_op jit(solution)/shard_map/tf,td->fd/dot_general | solution.py:453
  476.8 29.2 %all-to-all-start.3 = ((bf16[2,512,768]{2,0,1:T(2,128)(2,1)}), bf16[2,512,768]{2,0,1:T(2,128)(2,1)}, u32[]{:S(2)}, u32[]{:S(2)}) async-start(bf16[2,512,768]{2,0,1:T(2,128)(2,1)} %copy.143), calls=%async_computation.3 | async-start | bytes 3145728 | tf_op jit(solution)/shard_map/all_to_all | solution.py:328
  539.0 5.1 collective-permute-done.8
  547.3 6.3 collective-permute-done.9
  587.1 11.9 %collective-permute-done.11 = bf16[2,2,2,48,768]{4,3,1,2,0:T(8,128)(2,1)S(1)} collective-permute-done((bf16[2,2,2,48,768]{4,3,1,2,0:T(8,128)(2,1)S(1)}, bf16[2,2,2,48,768]{4,3,1,2,0:T(8,128)(2,1)S(1)}, u32[]{:S(2)}, u32[]{:S(2)}) %collective-permute-start.11) | collective-permute-done | bytes 589856 | tf_op jit(solution)/shard_map/ppermute | solution.py:278
  620.6 4.2 all-to-all-start.1
  632.2 7.1 %collective-permute-done.21 = bf16[2,2,2,24,3072]{4,3,1,2,0:T(8,128)(2,1)} collective-permute-done((bf16[2,2,2,24,3072]{4,3,1,2,0:T(8,128)(2,1)}, bf16[2,2,2,24,3072]{4,3,1,2,0:T(8,128)(2,1)}, u32[]{:S(2)}, u32[]{:S(2)}) %collective-permute-start.21) | collective-permute-done | bytes 1179680 | tf_op jit(solution)/shard_map/ppermute | solution.py:278
  642.7 4.2 convert_bitcast_fusion
  646.9 7.8 %all-to-all-done.1 = bf16[2,512,768]{2,0,1:T(2,128)(2,1)S(1)} async-done(((bf16[2,512,768]{2,0,1:T(2,128)(2,1)}), bf16[2,512,768]{2,0,1:T(2,128)(2,1)S(1)}, u32[]{:S(2)}, u32[]{:S(2)}) %all-to-all-start.1) | async-done | bytes 1572896 | tf_op jit(solution)/shard_map/all_to_all | solution.py:328
  667.3 4.6 collective-permute-done.27
  672.1 4.7 collective-permute-done.23
  681.1 6.7 collective-permute-done.24
  (445 shorter events, 192.1 us)
Async XLA Ops:
  0.8 43.4 %all-to-all-start = ((bf16[8,128,768]{2,1,0:T(8,128)(2,1)}), bf16[8,128,768]{2,1,0:T(8,128)(2,1)S(1)}, u32[]{:S(2)}, u32[]{:S(2)}) async-start(bf16[8,128,768]{2,1,0:T(8,128)(2,1)} %param.27), calls=%async_computation | async-start | bytes 3145728 | tf_op jit(solution)/shard_map/all_to_all | solution.py:370
  45.5 163.3 %all-to-all-start.2 = ((bf16[8,128,768]{2,1,0:T(8,128)(2,1)}), bf16[8,128,768]{2,1,0:T(8,128)(2,1)}, u32[]{:S(2)}, u32[]{:S(2)}) async-start(bf16[8,128,768]{2,1,0:T(8,128)(2,1)} %param.52), calls=%async_computation.2 | async-start | bytes 3145728 | tf_op jit(solution)/shard_map/all_to_all | solution.py:373
  476.8 143.9 %all-to-all-start.3 = ((bf16[2,512,768]{2,0,1:T(2,128)(2,1)}), bf16[2,512,768]{2,0,1:T(2,128)(2,1)}, u32[]{:S(2)}, u32[]{:S(2)}) async-start(bf16[2,512,768]{2,0,1:T(2,128)(2,1)} %copy.143), calls=%async_computation.3 | async-start | bytes 3145728 | tf_op jit(solution)/shard_map/all_to_all | solution.py:328
  512.9 57.9 %collective-permute-start = (bf16[2,2,2,2,32,768]{5,4,3,2,1,0:T(8,128)(2,1)}, bf16[2,2,2,2,32,768]{5,4,3,2,1,0:T(8,128)(2,1)}, u32[]{:S(2)}, u32[]{:S(2)}) collective-permute-start(bf16[2,2,2,2,32,768]{5,4,3,2,1,0:T(8,128)(2,1)} %fusion.34), channel_id=1, source_target_pairs={{0,4},{4,0},{8,12},{12,8},{16,20},{20,16},{24,28},{28,24},{1,5},{5... | collective-permute-start | bytes 2359304 | tf_op jit(solution)/shard_map/ppermute | solution.py:278
  521.2 23.0 %collective-permute-start.15 = (bf16[2,2,2,2,24,768]{5,4,3,2,1,0:T(8,128)(2,1)S(1)}, bf16[2,2,2,2,24,768]{5,4,3,2,1,0:T(8,128)(2,1)S(1)}, u32[]{:S(2)}, u32[]{:S(2)}) collective-permute-start(bf16[2,2,2,2,24,768]{5,4,3,2,1,0:T(8,128)(2,1)S(1)} %fusion.36), channel_id=1, source_target_pairs={{0,4},{4,0},{8,12},{12,8},{16,20},{20,16},{24,28},{28,24},{1,5},{5... | collective-permute-start | bytes 1769480 | tf_op jit(solution)/shard_map/ppermute | solution.py:278
  523.3 58.4 %collective-permute-start.10 = (bf16[2,2,2,2,48,768]{5,4,2,3,1,0:T(8,128)(2,1)}, bf16[2,2,2,2,48,768]{5,4,2,3,1,0:T(8,128)(2,1)}, u32[]{:S(2)}, u32[]{:S(2)}) collective-permute-start(bf16[2,2,2,2,48,768]{5,4,2,3,1,0:T(8,128)(2,1)} %fusion.33), channel_id=1, source_target_pairs={{0,4},{4,0},{8,12},{12,8},{16,20},{20,16},{24,28},{28,24},{1,5},{5... | collective-permute-start | bytes 3538952 | tf_op jit(solution)/shard_map/ppermute | solution.py:278
  531.9 80.9 %collective-permute-start.20 = (bf16[2,2,2,2,24,3072]{5,4,2,3,1,0:T(8,128)(2,1)}, bf16[2,2,2,2,24,3072]{5,4,2,3,1,0:T(8,128)(2,1)}, u32[]{:S(2)}, u32[]{:S(2)}) collective-permute-start(bf16[2,2,2,2,24,3072]{5,4,2,3,1,0:T(8,128)(2,1)} %fusion.15), channel_id=1, source_target_pairs={{0,4},{4,0},{8,12},{12,8},{16,20},{20,16},{24,28},{28,24},{1,5},{5... | collective-permute-start | bytes 7077896 | tf_op jit(solution)/shard_map/ppermute | solution.py:278
  532.7 11.4 %collective-permute-start.8 = (f32[40,768]{1,0:T(8,128)S(1)}, f32[40,768]{1,0:T(8,128)S(1)}, u32[]{:S(2)}, u32[]{:S(2)}) collective-permute-start(f32[40,768]{1,0:T(8,128)S(1)} %add.413), channel_id=1, source_target_pairs={{0,1},{1,0},{2,3},{3,2},{4,5},{5,4},{6,7},{7,6},{8,9},{9,8},{10,11... | collective-permute-start | bytes 368648 | tf_op jit(solution)/shard_map/ppermute | solution.py:278
  544.2 81.4 %collective-permute-start.25 = (bf16[2,2,2,2,96,768]{5,4,2,3,0,1:T(8,128)(2,1)}, bf16[2,2,2,2,96,768]{5,4,2,3,0,1:T(8,128)(2,1)}, u32[]{:S(2)}, u32[]{:S(2)}) collective-permute-start(bf16[2,2,2,2,96,768]{5,4,2,3,0,1:T(8,128)(2,1)} %fusion.16), channel_id=1, source_target_pairs={{0,4},{4,0},{8,12},{12,8},{16,20},{20,16},{24,28},{28,24},{1,5},{5... | collective-permute-start | bytes 7077896 | tf_op jit(solution)/shard_map/ppermute | solution.py:278
  544.2 9.3 %collective-permute-start.9 = (f32[40,768]{1,0:T(8,128)S(1)}, f32[40,768]{1,0:T(8,128)S(1)}, u32[]{:S(2)}, u32[]{:S(2)}) collective-permute-start(f32[40,768]{1,0:T(8,128)S(1)} %add.414), channel_id=1, source_target_pairs={{0,2},{1,3},{2,0},{3,1},{4,6},{5,7},{6,4},{7,5},{8,10},{9,11},{10,... | collective-permute-start | bytes 368648 | tf_op jit(solution)/shard_map/ppermute | solution.py:278
  553.5 15.7 %collective-permute-start.16 = (bf16[2,2,2,24,768]{4,3,2,1,0:T(8,128)(2,1)}, bf16[2,2,2,24,768]{4,3,2,1,0:T(8,128)(2,1)}, u32[]{:S(2)}, u32[]{:S(2)}) collective-permute-start(bf16[2,2,2,24,768]{4,3,2,1,0:T(8,128)(2,1)} %fusion.46), channel_id=1, source_target_pairs={{0,8},{4,12},{8,0},{12,4},{16,24},{20,28},{24,16},{28,20},{1,9},{5... | collective-permute-start | bytes 884744 | tf_op jit(solution)/shard_map/ppermute | solution.py:278
  576.4 9.9 %collective-permute-start.1 = (bf16[2,2,2,32,768]{4,3,2,1,0:T(8,128)(2,1)S(1)}, bf16[2,2,2,32,768]{4,3,2,1,0:T(8,128)(2,1)S(1)}, u32[]{:S(2)}, u32[]{:S(2)}) collective-permute-start(bf16[2,2,2,32,768]{4,3,2,1,0:T(8,128)(2,1)S(1)} %fusion.41), channel_id=1, source_target_pairs={{0,8},{4,12},{8,0},{12,4},{16,24},{20,28},{24,16},{28,20},{1,9},{5... | collective-permute-start | bytes 1179656 | tf_op jit(solution)/shard_map/ppermute | solution.py:278
  583.5 15.5 %collective-permute-start.11 = (bf16[2,2,2,48,768]{4,3,1,2,0:T(8,128)(2,1)S(1)}, bf16[2,2,2,48,768]{4,3,1,2,0:T(8,128)(2,1)S(1)}, u32[]{:S(2)}, u32[]{:S(2)}) collective-permute-start(bf16[2,2,2,48,768]{4,3,1,2,0:T(8,128)(2,1)S(1)} %fusion.35), channel_id=1, source_target_pairs={{0,16},{4,20},{8,24},{12,28},{16,0},{20,4},{24,8},{28,12},{1,17},{... | collective-permute-start | bytes 1769480 | tf_op jit(solution)/shard_map/ppermute | solution.py:278
  586.5 14.7 %collective-permute-start.2 = (bf16[2,2,32,768]{3,2,1,0:T(8,128)(2,1)S(1)}, bf16[2,2,32,768]{3,2,1,0:T(8,128)(2,1)S(1)}, u32[]{:S(2)}, u32[]{:S(2)}) collective-permute-start(bf16[2,2,32,768]{3,2,1,0:T(8,128)(2,1)S(1)} %fusion.49), channel_id=1, source_target_pairs={{0,16},{4,20},{8,24},{12,28},{16,0},{20,4},{24,8},{28,12},{1,17},{... | collective-permute-start | bytes 589832 | tf_op jit(solution)/shard_map/ppermute | solution.py:278
  607.9 11.5 %collective-permute-start.4 = (bf16[32,768]{1,0:T(8,128)(2,1)S(1)}, bf16[32,768]{1,0:T(8,128)(2,1)S(1)}, u32[]{:S(2)}, u32[]{:S(2)}) collective-permute-start(bf16[32,768]{1,0:T(8,128)(2,1)S(1)} %fusion.63), channel_id=1, source_target_pairs={{0,2},{1,3},{2,0},{3,1},{4,6},{5,7},{6,4},{7,5},{8,10},{9,11},{10,... | collective-permute-start | bytes 147464 | tf_op jit(solution)/shard_map/ppermute | solution.py:278
  611.3 13.5 %collective-permute-start.14 = (bf16[48,768]{1,0:T(8,128)(2,1)S(1)}, bf16[48,768]{1,0:T(8,128)(2,1)S(1)}, u32[]{:S(2)}, u32[]{:S(2)}) collective-permute-start(bf16[48,768]{1,0:T(8,128)(2,1)S(1)} %fusion.58), channel_id=1, source_target_pairs={{0,2},{1,3},{2,0},{3,1},{4,6},{5,7},{6,4},{7,5},{8,10},{9,11},{10,... | collective-permute-start | bytes 221192 | tf_op jit(solution)/shard_map/ppermute | solution.py:278
  618.8 20.6 %collective-permute-start.21 = (bf16[2,2,2,24,3072]{4,3,1,2,0:T(8,128)(2,1)}, bf16[2,2,2,24,3072]{4,3,1,2,0:T(8,128)(2,1)}, u32[]{:S(2)}, u32[]{:S(2)}) collective-permute-start(bf16[2,2,2,24,3072]{4,3,1,2,0:T(8,128)(2,1)} %fusion.31), channel_id=1, source_target_pairs={{0,16},{4,20},{8,24},{12,28},{16,0},{20,4},{24,8},{28,12},{1,17},{... | collective-permute-start | bytes 3538952 | tf_op jit(solution)/shard_map/ppermute | solution.py:278
  620.6 34.1 %all-to-all-start.1 = ((bf16[2,512,768]{2,0,1:T(2,128)(2,1)}), bf16[2,512,768]{2,0,1:T(2,128)(2,1)S(1)}, u32[]{:S(2)}, u32[]{:S(2)}) async-start(bf16[2,512,768]{2,0,1:T(2,128)(2,1)} %copy.137), calls=%async_computation.1 | async-start | bytes 3145728 | tf_op jit(solution)/shard_map/all_to_all | solution.py:328
  630.8 28.4 %collective-permute-start.26 = (bf16[2,2,2,96,768]{4,3,1,2,0:T(8,128)(2,1)}, bf16[2,2,2,96,768]{4,3,1,2,0:T(8,128)(2,1)}, u32[]{:S(2)}, u32[]{:S(2)}) collective-permute-start(bf16[2,2,2,96,768]{4,3,1,2,0:T(8,128)(2,1)} %fusion.32), channel_id=1, source_target_pairs={{0,8},{4,12},{8,0},{12,4},{16,24},{20,28},{24,16},{28,20},{1,9},{5... | collective-permute-start | bytes 3538952 | tf_op jit(solution)/shard_map/ppermute | solution.py:278
  642.0 22.2 %collective-permute-start.22 = (bf16[2,2,24,3072]{3,2,0,1:T(8,128)(2,1)}, bf16[2,2,24,3072]{3,2,0,1:T(8,128)(2,1)}, u32[]{:S(2)}, u32[]{:S(2)}) collective-permute-start(bf16[2,2,24,3072]{3,2,0,1:T(8,128)(2,1)} %fusion.37), channel_id=1, source_target_pairs={{0,8},{4,12},{8,0},{12,4},{16,24},{20,28},{24,16},{28,20},{1,9},{5... | collective-permute-start | bytes 1769480 | tf_op jit(solution)/shard_map/ppermute | solution.py:278
  661.0 10.8 %collective-permute-start.27 = (bf16[2,2,96,768]{3,2,0,1:T(8,128)(2,1)S(1)}, bf16[2,2,96,768]{3,2,0,1:T(8,128)(2,1)S(1)}, u32[]{:S(2)}, u32[]{:S(2)}) collective-permute-start(bf16[2,2,96,768]{3,2,0,1:T(8,128)(2,1)S(1)} %fusion.38), channel_id=1, source_target_pairs={{0,16},{4,20},{8,24},{12,28},{16,0},{20,4},{24,8},{28,12},{1,17},{... | collective-permute-start | bytes 1769480 | tf_op jit(solution)/shard_map/ppermute | solution.py:278
  665.4 11.3 %collective-permute-start.23 = (bf16[2,24,3072]{2,1,0:T(8,128)(2,1)S(1)}, bf16[2,24,3072]{2,1,0:T(8,128)(2,1)S(1)}, u32[]{:S(2)}, u32[]{:S(2)}) collective-permute-start(bf16[2,24,3072]{2,1,0:T(8,128)(2,1)S(1)} %fusion.47), channel_id=1, source_target_pairs={{0,1},{1,0},{2,3},{3,2},{4,5},{5,4},{6,7},{7,6},{8,9},{9,8},{10,11... | collective-permute-start | bytes 884744 | tf_op jit(solution)/shard_map/ppermute | solution.py:278
  676.9 10.9 %collective-permute-start.24 = (bf16[24,3072]{1,0:T(8,128)(2,1)S(1)}, bf16[24,3072]{1,0:T(8,128)(2,1)S(1)}, u32[]{:S(2)}, u32[]{:S(2)}) collective-permute-start(bf16[24,3072]{1,0:T(8,128)(2,1)S(1)} %fusion.52), channel_id=1, source_target_pairs={{0,2},{1,3},{2,0},{3,1},{4,6},{5,7},{6,4},{7,5},{8,10},{9,11},{10,... | collective-permute-start | bytes 442376 | tf_op jit(solution)/shard_map/ppermute | solution.py:278
  680.2 9.2 %collective-permute-start.29 = (bf16[96,768]{1,0:T(8,128)(2,1)S(1)}, bf16[96,768]{1,0:T(8,128)(2,1)S(1)}, u32[]{:S(2)}, u32[]{:S(2)}) collective-permute-start(bf16[96,768]{1,0:T(8,128)(2,1)S(1)} %fusion.53), channel_id=1, source_target_pairs={{0,2},{1,3},{2,0},{3,1},{4,6},{5,7},{6,4},{7,5},{8,10},{9,11},{10,... | collective-permute-start | bytes 442376 | tf_op jit(solution)/shard_map/ppermute | solution.py:278
  (120 other events, 1653.1 us)

commit v2 on v1

v2 whole, which is shorter than its diff:
```python
import functools
import math

import jax, jax.numpy as jnp
from jax import lax
from jax.experimental import pallas as pl
from jax.experimental.pallas import tpu as pltpu
from jax.sharding import PartitionSpec as P

HEADS = 12
RECEIPTS = 8
SPAN = 576
BINS = 160
NONE = -1e30
TALL = 192
WIDE = 256


def thresholds(half, reach):
    exact = half // 2
    steps = half - exact
    return [
        int(math.floor(exact * (reach / exact) ** (power / steps) + 0.5))
        for power in range(1, steps)
    ]


def bucket(diff, count, reach):
    half = count // 2
    exact = half // 2
    dist = jnp.abs(diff)
    passed = jnp.where(diff > 0, half, 0)
    for limit in thresholds(half, reach):
        passed = passed + jnp.where(dist >= limit, 1, 0)
    return passed + jnp.minimum(dist, exact)


def dot(a, b, ca, cb):
    return lax.dot_general(a, b, (((ca,), (cb,)), ((), ())), preferred_element_type=jnp.float32)


def by_size(bounds_ref, run, offset=0):
    step = pl.program_id(0) + offset * RECEIPTS
    receipt = lax.rem(step, RECEIPTS)
    base = step // RECEIPTS * 16 + receipt
    first = bounds_ref[base]
    last = bounds_ref[base + 1]
    start = first // 16 * 16
    for low, tall, wide in ((0, 64, 128), (64, 128, 128), (128, 192, 256)):
        inside = last - start > low
        if tall < TALL:
            inside = jnp.logical_and(inside, last - start <= tall)

        @pl.when(inside)
        def _(tall=tall, wide=wide):
            at_k = pl.multiple_of(jnp.minimum(start, SPAN - tall), 16)
            at_q = pl.multiple_of(jnp.minimum(start, SPAN - wide), 16)
            run(receipt, first - at_k, last - at_k, at_k, at_q, tall, wide)


def bias_kernel(bounds_ref, col_ref, row_ref, plane_ref, lines_ref, bias_ref, index_ref):
    def run(receipt, low, high, at_k, at_q, tall, wide):
        row = pltpu.roll(row_ref[0], lax.rem(640 - at_q, 640), 1)[:, :wide]
        height = 16

        def step(n, carry):
            at = pl.multiple_of(n * height, height)
            col = col_ref[0, pl.ds(pl.multiple_of(at_k + at, 16), height), :]
            shape = (height, 128)
            for c in range(wide // 128):
                lanes = slice(128 * c, 128 * (c + 1))

                def spread(r):
                    return (jnp.broadcast_to(col[:, r : r + 1], shape), jnp.broadcast_to(row[r : r + 1, lanes], shape))

                def gap(r):
                    key, query = spread(r)
                    return key - query

                key, query = spread(3)
                same = jnp.logical_and(key == receipt, query == receipt)
                line = jnp.where(same, bucket(gap(0), 32, 128), 32)
                across = bucket(gap(1), 64, 256)
                down = bucket(gap(2), 64, 256) + 64
                index_ref[0, pl.ds(at, height), lanes] = across + down * 256 + line * 65536
                for h in range(HEADS):
                    def look(ref, index):
                        table = jnp.broadcast_to(ref[h : h + 1, :], shape)
                        return jnp.take_along_axis(table, index, axis=1, mode="promise_in_bounds")

                    bias_ref[0, h, pl.ds(at, height), lanes] = (
                        look(plane_ref, across) + look(plane_ref, down) + look(lines_ref, line)
                    )
            return carry

        lax.fori_loop(0, tall // height, step, 0)

    by_size(bounds_ref, run)


def split_pair(value, scale=1.0):
    lane = lax.broadcasted_iota(jnp.int32, value.shape, 1)
    full = value.astype(jnp.float32) * scale
    low = jnp.where(lane < 64, full, 0.0).astype(value.dtype)
    high = jnp.where(lane < 64, 0.0, full).astype(value.dtype)
    return jnp.concatenate([low, high], axis=0)


def parts(pair, at_k, at_q, tall, wide):
    width = HEADS * 64
    return (
        (0, pl.ds(at_q, wide), pl.ds(128 * pair, 128)),
        (0, pl.ds(at_k, tall), pl.ds(width + 128 * pair, 128)),
        (0, pl.ds(at_k, tall), pl.ds(2 * width + 128 * pair, 128)),
    )


def gather_into(ref, where, value):
    ref[where] = (ref[where].astype(jnp.float32) + value).astype(ref.dtype)


def forward_kernel(bounds_ref, qkv_ref, row_ref, bias_ref, out_ref, shares_ref):
    @pl.when(lax.rem(pl.program_id(0), RECEIPTS) == 0)
    def _():
        out_ref[...] = jnp.zeros_like(out_ref)

    def run(receipt, low, high, at_k, at_q, tall, wide):
        owner = pltpu.roll(row_ref[0], lax.rem(640 - at_q, 640), 1)[3:4, :wide]
        mine = jnp.where(owner == receipt, 1.0, 0.0)
        for pair in range(HEADS // 2):
            queries, keys, values = parts(pair, at_k, at_q, tall, wide)
            scores = dot(split_pair(qkv_ref[keys], 0.125), qkv_ref[queries], 1, 1)
            halves = []
            for h in range(2):
                part = scores[h * tall : (h + 1) * tall] + bias_ref[0, 2 * pair + h, :tall, :wide]
                expo = jnp.exp(part - jnp.max(part, axis=0, keepdims=True))
                share = expo * (mine / jnp.sum(expo, axis=0, keepdims=True))
                halves.append(share.astype(jnp.bfloat16))
                shares_ref[0, 2 * pair + h, :tall, :wide] = halves[h]
            shares = jnp.concatenate(halves, axis=0)
            gather_into(out_ref, queries, dot(shares, split_pair(qkv_ref[values]), 0, 0))

    by_size(bounds_ref, run)


def backward_kernel(offset, bounds_ref, qkv_ref, g_ref, shares_ref, dqkv_ref, ds_ref):
    @pl.when(lax.rem(pl.program_id(0), RECEIPTS) == 0)
    def _():
        dqkv_ref[...] = jnp.zeros_like(dqkv_ref)

    def run(receipt, low, high, at_k, at_q, tall, wide):
        for pair in range(HEADS // 2):
            queries, keys, values = parts(pair, at_k, at_q, tall, wide)
            grad = g_ref[queries]
            grad_probs = dot(split_pair(qkv_ref[values]), grad, 1, 1)
            shares, steps = [], []
            for h in range(2):
                share = shares_ref[0, 2 * pair + h, :tall, :wide]
                part = grad_probs[h * tall : (h + 1) * tall]
                probs = share.astype(jnp.float32)
                inner = jnp.sum(probs * part, axis=0, keepdims=True)
                step = (probs * (part - inner)).astype(jnp.bfloat16)
                ds_ref[0, 2 * pair + h, :tall, :wide] = step
                shares.append(share)
                steps.append(step)
            gather_into(dqkv_ref, values, dot(jnp.concatenate(shares, axis=1), split_pair(grad), 1, 0))
            gather_into(dqkv_ref, keys, dot(jnp.concatenate(steps, axis=1), split_pair(qkv_ref[queries], 0.125), 1, 0))
            gather_into(dqkv_ref, queries, dot(jnp.concatenate(steps, axis=0), split_pair(qkv_ref[keys], 0.125), 0, 0))

    by_size(bounds_ref, run, offset)


def bins_kernel(offset, bounds_ref, index_ref, ds_ref, bins_ref, terms_s):
    @pl.when(pl.program_id(0) == 0)
    def _():
        bins_ref[...] = jnp.zeros_like(bins_ref)
        terms_s[...] = jnp.zeros_like(terms_s)

    group = 16

    def run(receipt, low, high, at_k, at_q, tall, wide):
        for h in range(HEADS):
            for c in range(wide // 128):
                terms_s[c, pl.ds(h, tall, stride=16), :] = ds_ref[0, h, :tall, 128 * c : 128 * c + 128].astype(jnp.float32)
        level = lax.broadcasted_iota(jnp.int32, (BINS, 128), 0)

        def step(n, total):
            hots, terms = [], []
            at = pl.multiple_of(n * group, group)
            for c in range(wide // 128):
                packed = index_ref[0, pl.ds(at, group), 128 * c : 128 * c + 128]
                x, y, line = packed & 255, (packed >> 8) & 255, (packed >> 16) + 128
                for i in range(group):
                    def spread(value, count):
                        return jnp.broadcast_to(value[i : i + 1, :], (count, 128))

                    index = jnp.concatenate([spread(x, 64), spread(y, 64), spread(line, 32)], axis=0)
                    hots.append(jnp.where(level == index, 1.0, 0.0).astype(jnp.bfloat16))
                    terms.append(terms_s[c, pl.ds(pl.multiple_of((at + i) * 16, 16), 16), :].astype(jnp.bfloat16))
            return total + dot(jnp.concatenate(hots, axis=1), jnp.concatenate(terms, axis=1), 1, 1)

        total = lax.fori_loop(low // group, pl.cdiv(high, group), step, jnp.zeros((BINS, 16), jnp.float32))
        bins_ref[:, :BINS] += total.T

    by_size(bounds_ref, run, offset)


def of_row(shape, offset=0):
    return pl.BlockSpec((1,) + shape, lambda n, *_: (n // RECEIPTS + offset,) + (0,) * len(shape))


def of_step(shape, offset=0):
    return pl.BlockSpec((1,) + shape, lambda n, *_: (n + offset * RECEIPTS,) + (0,) * len(shape))


def fixed(shape):
    return pl.BlockSpec(shape, lambda n, *_: (0,) * len(shape))


def call(kernel, name, bounds, args, in_specs, out_specs, out_shape, steps, cost, scratch=(), vmem=48):
    return pl.pallas_call(
        kernel,
        grid_spec=pltpu.PrefetchScalarGridSpec(
            num_scalar_prefetch=1, grid=(steps,), in_specs=in_specs, out_specs=out_specs, scratch_shapes=scratch
        ),
        out_shape=out_shape,
        compiler_params=pltpu.CompilerParams(vmem_limit_bytes=vmem * 1024 * 1024),
        cost_estimate=pl.CostEstimate(flops=cost, bytes_accessed=cost // 1000, transcendentals=0),
        name=name,
    )(bounds, *args)


def make_bias(bounds, col, row, plane, lines):
    steps = col.shape[0] * RECEIPTS
    return call(
        bias_kernel, "make_bias", bounds, (col, row, plane, lines),
        [of_row((SPAN, 128)), of_row((8, 640)), fixed((HEADS, 128)), fixed((HEADS, 128))],
        [of_step((HEADS, TALL, WIDE)), of_step((TALL, WIDE))],
        [jax.ShapeDtypeStruct((steps, HEADS, TALL, WIDE), jnp.float32), jax.ShapeDtypeStruct((steps, TALL, WIDE), jnp.int32)],
        steps, 30_000_000_000,
    )


def attend(bounds, qkv, row, bias):
    rows, span, width = qkv.shape
    steps = rows * RECEIPTS
    return call(
        forward_kernel, "attend", bounds, (qkv, row, bias),
        [of_row((span, width)), of_row((8, 640)), of_step((HEADS, TALL, WIDE))],
        [of_row((span, width // 3)), of_step((HEADS, TALL, WIDE))],
        [
            jax.ShapeDtypeStruct((rows, span, width // 3), qkv.dtype),
            jax.ShapeDtypeStruct((steps, HEADS, TALL, WIDE), jnp.bfloat16),
        ],
        steps, 20_000_000_000,
    )


def attend_back(bounds, qkv, g, shares, first):
    rows, span, width = qkv.shape
    return call(
        functools.partial(backward_kernel, first), "attend_back", bounds, (qkv, g, shares),
        [of_row((span, width), first), of_row((span, width // 3), first), of_step((HEADS, TALL, WIDE), first)],
        [of_row((span, width)), of_step((HEADS, TALL, WIDE))],
        [
            jax.ShapeDtypeStruct((1, span, width), qkv.dtype),
            jax.ShapeDtypeStruct((RECEIPTS, HEADS, TALL, WIDE), jnp.bfloat16),
        ],
        RECEIPTS, 12_000_000_000,
    )


def make_bins(bounds, index, grads, first):
    out = (16, HEADS * 64)
    return call(
        functools.partial(bins_kernel, first), "make_bins", bounds, (index, grads),
        [of_step((TALL, WIDE), first), of_step((HEADS, TALL, WIDE))],
        fixed(out),
        jax.ShapeDtypeStruct(out, jnp.float32),
        RECEIPTS, 12_000_000_000, [pltpu.VMEM((2, TALL * 16, 128), jnp.float32)],
    )


EPSILON = 1e-05


def gelu_parts(u):
    expo = jnp.exp(u * u * -0.5)
    share = 0.5 + 0.5 * lax.erf(u * (1.0 / math.sqrt(2.0)))
    return u * share, share + u * expo * (1.0 / math.sqrt(2.0 * math.pi))


def standard(values):
    centred = values - jnp.mean(values, axis=1, keepdims=True)
    scale = lax.rsqrt(jnp.mean(centred * centred, axis=1, keepdims=True) + EPSILON)
    return centred * scale, scale


def standard_back(normed, scale, grad):
    return (
        grad - jnp.mean(grad, axis=1, keepdims=True) - normed * jnp.mean(grad * normed, axis=1, keepdims=True)
    ) * scale


def total(value):
    return jnp.sum(value, axis=0, keepdims=True)


def up_kernel(
    context_ref, stream_ref, cot_ref, w_out_ref, w_up_ref, w_down_ref, rows_ref, b_up_ref,
    mid_ref, hidden_ref, active_ref, slope_ref, out_ref, top_ref, branch_ref, sums_ref, *, chunk,
):
    b_out, gain_1, shift_1, b_down, gain_2, shift_2 = (rows_ref[n : n + 1, :] for n in range(6))
    mid = stream_ref[...] + dot(context_ref[...], w_out_ref[...], 1, 0) + b_out
    mid_ref[...] = mid
    norm_one = standard(mid)[0] * gain_1 + shift_1
    hidden = norm_one.astype(jnp.bfloat16)
    hidden_ref[...] = hidden
    branch = norm_one + b_down
    for at in range(0, w_up_ref.shape[1], chunk):
        piece = slice(at, at + chunk)
        inner = dot(hidden, w_up_ref[:, piece], 1, 0) + b_up_ref[:, piece]
        active, slope = gelu_parts(inner)
        active = active.astype(jnp.bfloat16)
        active_ref[:, piece] = active
        slope_ref[:, piece] = slope.astype(jnp.bfloat16)
        branch = branch + dot(active, w_down_ref[piece, :], 1, 0)
    normed, scale = standard(branch)
    out_ref[...] = (normed * gain_2 + shift_2).astype(jnp.bfloat16)
    cot = cot_ref[...].astype(jnp.float32)
    top = standard_back(normed, scale, cot * gain_2)
    top_ref[...] = top
    low = top.astype(jnp.bfloat16)
    branch_ref[...] = low

    @pl.when(pl.program_id(0) == 0)
    def _():
        sums_ref[...] = jnp.zeros_like(sums_ref)

    sums_ref[0:1, :] += total(cot * normed)
    sums_ref[1:2, :] += total(cot)
    sums_ref[2:3, :] += total(low.astype(jnp.float32))


def down_kernel(
    branch_ref, slope_ref, top_ref, mid_ref, w_out_ref, w_up_ref, w_down_ref, rows_ref,
    inner_ref, mid_grad_ref, attended_ref, context_ref, sums_ref, ups_ref, *, chunk,
):
    @pl.when(pl.program_id(0) == 0)
    def _():
        sums_ref[...] = jnp.zeros_like(sums_ref)
        ups_ref[...] = jnp.zeros_like(ups_ref)

    gain_1 = rows_ref[1:2, :]
    branch = branch_ref[...]
    grad = top_ref[...]
    for at in range(0, w_up_ref.shape[1], chunk):
        piece = slice(at, at + chunk)
        inner = dot(branch, w_down_ref[piece, :], 1, 1) * slope_ref[:, piece].astype(jnp.float32)
        low = inner.astype(jnp.bfloat16)
        inner_ref[:, piece] = low
        ups_ref[0:1, piece] += total(low.astype(jnp.float32))
        grad = grad + dot(low, w_up_ref[:, piece], 1, 1)
    normed, scale = standard(mid_ref[...])
    back = standard_back(normed, scale, grad * gain_1)
    mid_grad_ref[...] = back
    low = back.astype(jnp.bfloat16)
    attended_ref[...] = low
    context_ref[...] = dot(low, w_out_ref[...], 1, 1).astype(jnp.bfloat16)
    sums_ref[0:1, :] += total(grad * normed)
    sums_ref[1:2, :] += total(grad)
    sums_ref[2:3, :] += total(low.astype(jnp.float32))


def tiled(tile, width):
    return pl.BlockSpec((tile, width), lambda n: (n, 0))


def whole(shape):
    return pl.BlockSpec(shape, lambda n: (0, 0))


def feed_forward(context, stream_in, cot, w_out, w_up, w_down, vectors, b_up, tile=384, chunk=512):
    tokens, width = context.shape
    deep = w_up.shape[1]
    low, full = jnp.bfloat16, jnp.float32
    shapes = [(width, full), (width, low), (deep, low), (deep, low), (width, low), (width, full), (width, low)]
    return pl.pallas_call(
        functools.partial(up_kernel, chunk=chunk),
        grid=(tokens // tile,),
        in_specs=[tiled(tile, width)] * 3
        + [whole(w_out.shape), whole(w_up.shape), whole(w_down.shape), whole(vectors.shape), whole(b_up.shape)],
        out_specs=[tiled(tile, n) for n, _ in shapes] + [whole((8, width))],
        out_shape=[jax.ShapeDtypeStruct((tokens, n), kind) for n, kind in shapes]
        + [jax.ShapeDtypeStruct((8, width), full)],
        compiler_params=pltpu.CompilerParams(vmem_limit_bytes=60 * 1024 * 1024),
        cost_estimate=pl.CostEstimate(flops=20_000_000_000, bytes_accessed=60_000_000, transcendentals=0),
        name="feed_forward",
    )(context, stream_in, cot, w_out, w_up, w_down, vectors, b_up)


def feed_back(branch, slope, top, mid, w_out, w_up, w_down, vectors, tile=384, chunk=512):
    tokens, width = branch.shape
    deep = w_up.shape[1]
    low, full = jnp.bfloat16, jnp.float32
    shapes = [(deep, low), (width, full), (width, low), (width, low)]
    return pl.pallas_call(
        functools.partial(down_kernel, chunk=chunk),
        grid=(tokens // tile,),
        in_specs=[tiled(tile, width), tiled(tile, deep), tiled(tile, width), tiled(tile, width)]
        + [whole(w_out.shape), whole(w_up.shape), whole(w_down.shape), whole(vectors.shape)],
        out_specs=[tiled(tile, n) for n, _ in shapes] + [whole((8, width)), whole((8, deep))],
        out_shape=[jax.ShapeDtypeStruct((tokens, n), kind) for n, kind in shapes]
        + [jax.ShapeDtypeStruct((8, width), full), jax.ShapeDtypeStruct((8, deep), full)],
        compiler_params=pltpu.CompilerParams(vmem_limit_bytes=60 * 1024 * 1024),
        cost_estimate=pl.CostEstimate(flops=20_000_000_000, bytes_accessed=60_000_000, transcendentals=0),
        name="feed_back",
    )(branch, slope, top, mid, w_out, w_up, w_down, vectors)


DP = "dp"
STREAM = "stream"


def swap(value, axis, bit):
    count = lax.axis_size(axis)
    return lax.ppermute(value, axis, [(i, i ^ bit) for i in range(count)])


def bits_of(axis):
    count = lax.axis_size(axis)
    return [1 << n for n in range(count.bit_length() - 1)]


def stages(flip):
    core, *chips = bits_of(DP)
    if flip:
        chips = chips[::-1]
    return [(DP, core)] + [(DP, bit) for bit in chips] + [(STREAM, bit) for bit in bits_of(STREAM)]


class Scatter:
    def __init__(self, values, flip):
        self.names = [(axis, bit) for axis in (DP, STREAM) for bit in bits_of(axis)[::-1]]
        self.values = [value.reshape((2,) * len(self.names) + value.shape[1:]) for value in values]
        self.left = stages(flip)

    def send(self):
        stage = self.left.pop(0)
        axis, bit = stage
        dim = self.names.index(stage)
        self.names.pop(dim)
        side = (lax.axis_index(axis) // bit) % 2

        def pick(value, n):
            return lax.dynamic_index_in_dim(value, n, dim, keepdims=False)

        given = jnp.concatenate([pick(value, 1 - side).astype(jnp.bfloat16) for value in self.values], axis=-1)
        self.kept = [pick(value, side) for value in self.values]
        self.got = swap(given, axis, bit)

    def add(self):
        if self.got is None:
            return
        self.values, at = [], 0
        for kept in self.kept:
            got = self.got[..., at : at + kept.shape[-1]]
            at += kept.shape[-1]
            self.values.append(kept + got.astype(jnp.float32))
        self.got = None

    def next(self):
        self.add()
        if self.left:
            self.send()

    def after(self, other):
        if self.got is None:
            return other
        other, self.got = lax.optimization_barrier((other, self.got))
        return other

    def finish(self):
        while self.left:
            self.next()
        self.add()
        return self.values


def together(*values):
    return lax.optimization_barrier(values)


def sum_all(value):
    for axis, bit in stages(False):
        value = value + swap(value, axis, bit)
    return value


def turned(shift):
    count = lax.axis_size(STREAM)
    return [(i, (i + shift) % count) for i in range(count)]


def to_rows(value):
    count = lax.axis_size(STREAM)
    place = lax.axis_index(STREAM)
    block = value.shape[0] // count
    parts = []
    for shift in range(count):
        part = lax.dynamic_slice_in_dim(value, (place - shift) % count * block, block, 0)
        parts.append(lax.ppermute(part, STREAM, turned(-shift)) if shift else part)
    return jnp.concatenate(parts, axis=1)


def slot_sends(value):
    count = lax.axis_size(STREAM)
    block = value.shape[0] // count
    parts = [value[shift * block : (shift + 1) * block] for shift in range(count)]
    return parts[:1] + [lax.ppermute(parts[shift], STREAM, turned(shift)) for shift in range(1, count)]


def from_sends(rows, dtype):
    count = lax.axis_size(STREAM)
    place = lax.axis_index(STREAM)
    whole = jnp.zeros((len(rows) * count,) + rows[0][0].shape, dtype)
    for at, parts in enumerate(rows):
        for shift, part in enumerate(parts):
            whole = lax.dynamic_update_slice_in_dim(
                whole, part[None].astype(dtype), (place - shift) % count * len(rows) + at, 0
            )
    return whole


def per_device(
    text_input,
    visual_features,
    receipt_text,
    receipt_visual,
    boxes,
    w_query,
    b_query,
    w_key,
    w_value,
    b_value,
    w_out,
    b_out,
    gain_attn,
    shift_attn,
    w_up,
    b_up,
    w_down,
    b_down,
    gain_ffn,
    shift_ffn,
    w_visual,
    b_visual,
    table_line,
    table_x,
    table_y,
    cotangent_text,
    cotangent_visual,
):
    floating = jnp.float32
    narrow = jnp.bfloat16
    width = text_input.shape[-1]
    rows, visual, channels = visual_features.shape
    text = receipt_text.shape[1]
    slots = text + visual
    world = lax.axis_size(DP) * lax.axis_size(STREAM)
    place = lax.axis_index(STREAM)
    first_row = place * rows

    text_rows = to_rows(text_input)
    text_rows, cotangent_text = lax.optimization_barrier((text_rows, cotangent_text))
    cotangent_rows = to_rows(cotangent_text)

    def pad(value, fill=0):
        extra = SPAN - value.shape[1]
        return jnp.pad(value, ((0, 0), (0, extra)) + ((0, 0),) * (value.ndim - 2), constant_values=fill)

    seg_text = lax.dynamic_slice_in_dim(receipt_text, first_row, rows, 0)
    seg_visual = lax.dynamic_slice_in_dim(receipt_visual, first_row, rows, 0)
    box = lax.dynamic_slice_in_dim(boxes, first_row, rows, 1)
    index = jnp.arange(SPAN, dtype=jnp.int32)
    position = jnp.where(index < text, index, index - text)
    facts = jnp.stack(
        [
            jnp.broadcast_to(position, (rows, SPAN)),
            pad(box[0]),
            pad(box[1]),
            pad(jnp.concatenate([seg_text, seg_visual], axis=1), RECEIPTS),
            jnp.broadcast_to(index, (rows, SPAN)),
        ],
        axis=1,
    )
    own = lax.dynamic_slice_in_dim(
        jnp.concatenate([facts[:, :, :text], facts[:, :, :text]], axis=2), place * text_input.shape[1], text, 2
    )
    facts = jnp.concatenate([own, facts[:, :, text:]], axis=2)
    rank = facts[:, 3] * SPAN + facts[:, 4]
    seg = facts[:, 3]
    target = jnp.sum((rank[:, None, :] < rank[:, :, None]).astype(jnp.int32), axis=2)
    moved = target[:, None, :] == index[None, :, None]
    facts = facts[:, :4]
    facts = jnp.sum(jnp.where(moved[:, None], facts[:, :, None, :], 0), axis=3)
    col = jnp.pad(jnp.swapaxes(facts, 1, 2), ((0, 0), (0, 0), (0, 124)))
    row = jnp.pad(facts, ((0, 0), (0, 4), (0, 640 - SPAN)), constant_values=RECEIPTS)
    bounds = jnp.sum(
        (seg[:, None, :] < jnp.arange(16, dtype=jnp.int32)[None, :, None]).astype(jnp.int32), axis=2
    ).reshape(-1)
    plane = jnp.concatenate([table_x, table_y], axis=1).astype(floating)
    lines = jnp.pad(table_line.astype(floating), ((0, 0), (0, 96)), constant_values=NONE)

    bias, places = make_bias(bounds, col, row, plane, lines)
    moving = moved.astype(narrow)

    def sort(value):
        return jnp.einsum("rps,rsd->rpd", moving[:, :, : value.shape[1]], value, preferred_element_type=floating)

    def unsort(value):
        return jnp.einsum("rps,rpd->rsd", moving, value, preferred_element_type=floating)

    def rowwise(array):
        return array.reshape(rows, SPAN, -1)

    w_qkv = jnp.concatenate([w_query, w_key, w_value], axis=1)
    b_qkv = jnp.concatenate([b_query, jnp.zeros_like(b_query), b_value]).astype(floating)
    features = jnp.einsum(
        "rpv,rvc->rpc", moving[:, :, text:slots], visual_features, preferred_element_type=floating
    ).astype(narrow)
    is_visual = jnp.sum(moving[:, :, text:slots].astype(floating), axis=2)[:, :, None]
    features_flat = features.reshape(-1, channels)
    visual_pre = jnp.einsum("rpc,cd->rpd", features, w_visual, preferred_element_type=floating)
    visual_pre = (visual_pre + b_visual.astype(floating)) * is_visual
    stream_in = (sort(text_rows) + visual_pre).reshape(-1, width)
    entered = stream_in.astype(narrow)
    qkv = rowwise((jnp.dot(entered, w_qkv, preferred_element_type=floating) + b_qkv).astype(narrow))
    context, shares = attend(bounds, qkv, row, bias)
    context, cotangent_rows = together(context, cotangent_rows)
    context = context.reshape(-1, width)
    cotangent = sort(jnp.concatenate([cotangent_rows, cotangent_visual], axis=1)).astype(narrow).reshape(-1, width)
    vectors = jnp.stack([b_out, gain_attn, shift_attn, b_down, gain_ffn, shift_ffn, b_out, b_out]).astype(floating)
    mid, hidden, active, slope, outcome, grad_top, grad_branch, ffn_sums = feed_forward(
        context, stream_in, cotangent, w_out, w_up, w_down, vectors, b_up.astype(floating)[None]
    )
    grad_w_down = jnp.einsum("tf,td->fd", active, grad_branch, preferred_element_type=floating)
    grad_w_down, grad_branch, outcome = together(grad_w_down, grad_branch, outcome)
    downs = Scatter([grad_w_down.reshape(world, -1, width)], False)
    downs.send()
    out_rows = unsort(rowwise(outcome)).astype(narrow)
    out_visual = out_rows[:, text:slots]
    grad_branch, out_rows = together(grad_branch, out_rows)
    grad_branch = downs.after(grad_branch)
    downs.next()
    out_sends = [slot_sends(out[:text]) for out in out_rows]
    grad_inner, grad_mid, grad_attended, grad_context, attn_sums, up_sums = feed_back(
        grad_branch, slope, grad_top, mid, w_out, w_up, w_down, vectors
    )
    grad_w_up = jnp.einsum("td,tf->df", hidden, grad_inner, preferred_element_type=floating)
    grad_w_out = jnp.einsum("td,te->de", context, grad_attended, preferred_element_type=floating)
    grad_context, grad_w_out, grad_w_up = together(grad_context, grad_w_out, grad_w_up)
    flat, tree = jax.tree.flatten(out_sends)
    grad_context, *flat = together(grad_context, *flat)
    out_text = from_sends(jax.tree.unflatten(tree, flat), narrow)
    ups = Scatter([part.reshape(world, width // world, -1) for part in (grad_w_up, grad_w_out)], True)
    ups.send()

    grad_context = rowwise(grad_context)
    entered_rows, grad_mid_rows = rowwise(entered), rowwise(grad_mid)

    def advance(value, groups, extra=()):
        tied = together(value, *extra, *(group.got for group in groups))
        for group, got in zip(groups, tied[1 + len(extra) :]):
            group.got = got
            group.next()
        return tied[0], list(tied[1 : 1 + len(extra)])

    def project(r, grad_qkv):
        grad_stream = grad_mid_rows[r] + jnp.einsum("te,de->td", grad_qkv, w_qkv, preferred_element_type=floating)
        (grad_low,) = together(grad_stream.astype(narrow))
        back = jnp.einsum("ps,pd->sd", moving[r], grad_low, preferred_element_type=floating).astype(narrow)
        grad_w = jnp.einsum("td,te->de", entered_rows[r], grad_qkv, preferred_element_type=floating)
        return back, grad_w, jnp.sum(grad_qkv, axis=0, dtype=floating)

    grad_qkv, step_0 = attend_back(bounds, qkv, grad_context, shares, 0)
    grad_qkv, _ = advance(grad_qkv[0], [downs, ups])
    back_0, grad_w_qkv, grad_b_qkv = project(0, grad_qkv)
    got_0 = slot_sends(back_0[:text])
    grad_context, back_0, grad_w_qkv = together(grad_context, back_0, grad_w_qkv)
    grad_qkv, step_1 = attend_back(bounds, qkv, grad_context, shares, 1)
    grad_qkv, got_0 = advance(grad_qkv[0], [downs, ups], got_0)
    back_1, more_w, more_b = project(1, grad_qkv)
    got_1 = slot_sends(back_1[:text])
    grad_w_qkv, grad_b_qkv = grad_w_qkv + more_w, grad_b_qkv + more_b
    grad_visual = jnp.stack([back_0[text:slots], back_1[text:slots]])
    grad_w_visual = jnp.einsum("rvc,rvd->cd", visual_features, grad_visual, preferred_element_type=floating)
    grad_b_visual = jnp.sum(grad_visual, axis=(0, 1), dtype=floating)
    grad_features = jnp.einsum("rvd,cd->rvc", grad_visual, w_visual, preferred_element_type=floating)
    lasts = Scatter([part.reshape(world, width // world, -1) for part in (grad_w_qkv, grad_w_visual)], False)
    lasts.send()
    step_0, back_1, *lasts.kept = together(step_0, back_1, *lasts.kept)
    bins = make_bins(bounds, places, step_0, 0)
    bins, got_1 = advance(bins, [downs, ups, lasts], got_1)
    step_1, bins = together(step_1, bins)
    more = make_bins(bounds, places, step_1, 1)
    more, _ = advance(more, [group for group in (downs, ups, lasts) if group.got is not None])
    bins = bins + more
    grad_text = from_sends([got_0, got_1], floating)
    (down_sum,) = downs.finish()
    up_sum, out_sum = ups.finish()
    qkv_sum, visual_sum = lasts.finish()
    query_sum, key_sum, value_sum = (qkv_sum[:, n * width : (n + 1) * width] for n in range(3))
    visual_sum = visual_sum.reshape(-1, width)
    step = width // world
    def lines_of(value):
        return [value[:, n : n + width] for n in range(0, value.shape[1], width)]

    small = sum_all(
        jnp.concatenate(
            [ffn_sums, attn_sums, bins]
            + lines_of(grad_b_qkv[None]) + [grad_b_visual[None]] + lines_of(up_sums[:1]),
            axis=0,
        )
    )
    device = lax.axis_index(DP) * lax.axis_size(STREAM) + place
    mine = lax.dynamic_slice_in_dim(small, device * step, step, 1)
    up_step = w_up.shape[1] // world
    bins = small[16 : 16 + HEADS]
    return (
        out_text,
        out_visual,
        grad_text,
        grad_features,
        query_sum,
        mine[32],
        key_sum,
        value_sum,
        mine[34],
        out_sum,
        mine[10],
        mine[8],
        mine[9],
        up_sum,
        lax.dynamic_slice_in_dim(small[36:].reshape(-1), device * up_step, up_step, 0),
        down_sum,
        mine[2],
        mine[0],
        mine[1],
        visual_sum,
        mine[35],
        bins[:, 128:160],
        bins[:, :64],
        bins[:, 64:128],
    )


def solution(mesh):
    placed = (
        P("dp", "stream", None),
        P(("dp", "stream"), None, None),
        P("dp", None),
        P("dp", None),
        P(None, "dp", None),
        P(),
        P(),
        P(),
        P(),
        P(),
        P(),
        P(),
        P(),
        P(),
        P(),
        P(),
        P(),
        P(),
        P(),
        P(),
        P(),
        P(),
        P(),
        P(),
        P(),
        P("dp", "stream", None),
        P(("dp", "stream"), None, None),
    )
    return jax.shard_map(
        per_device,
        mesh=mesh,
        in_specs=placed,
        out_specs=(
            P("dp", "stream", None),
            P(("dp", "stream"), None, None),
            P("dp", "stream", None),
            P(("dp", "stream"), None, None),
            P(("dp", "stream"), None),
            P(("dp", "stream")),
            P(("dp", "stream"), None),
            P(("dp", "stream"), None),
            P(("dp", "stream")),
            P(("dp", "stream"), None),
            P(("dp", "stream")),
            P(("dp", "stream")),
            P(("dp", "stream")),
            P(("dp", "stream"), None),
            P(("dp", "stream")),
            P(("dp", "stream"), None),
            P(("dp", "stream")),
            P(("dp", "stream")),
            P(("dp", "stream")),
            P(("dp", "stream"), None),
            P(("dp", "stream")),
            P(),
            P(),
            P(),
        ),
        check_vma=False,
    )
```

time: 696 us -> 497 us (0.71)
  matrix products: 147 us -> 59.1 us
  waiting for transfers between devices: 99.7 us -> 57.7 us
  Pallas kernels: 257 us -> 223 us
  starting transfers between devices: 67.2 us -> 46 us
  local copies, waits for them, and re-layouts: 71.4 us -> 56.6 us
    dot_general x16 -> x8, matrix products: 119 us -> 32.4 us  [the longest x2 10.3 us: project(): jnp.einsum('td,te->de', entered_rows[r], grad_qkv, preferred_element_type...]
    all_to_all x4 -> x0, starting transfers between devices: 44.7 us -> none  [the longest x2 33.4 us: by_slots(): return lax.all_to_all(value, STREAM, 1, 0, tiled=True)]
    pallas_call x2 -> x8, Pallas kernels: 257 us -> 223 us  [the longest x6 168 us: call(): pl.pallas_call(kernel, grid_spec=pltpu.PrefetchScalarGridSpec(num_scalar_...]
    all_to_all x4 -> x0, waiting for transfers between devices: 28.2 us -> none  [the longest x1 20.3 us: per_device(): text_rows = lax.all_to_all(text_input, STREAM, 0, 1, tiled=True)]
    ppermute x0 -> x18, starting transfers between devices: none -> 24.3 us  [the longest x12 14.2 us: slot_sends(): lax.ppermute(parts[shift], STREAM, turned(shift))]
    ppermute x30 -> x20, waiting for transfers between devices: 71.5 us -> 51.7 us  [swap(): return lax.ppermute(value, axis, [(i, i ^ bit) for i in range(count)])]
    convert_element_type x25, local copies, waits for them, and re-layouts: 16.3 us -> 6.57 us  [send(): pick(value, 1 - side).astype(jnp.bfloat16)]
    convert_element_type x11 -> x2, other arithmetic: 9.36 us -> 0.62 us  [the longest x1 0.61 us: per_device(): jnp.stack([b_out, gain_attn, shift_attn, b_down, gain_ffn, shift_ffn, b_o...]
  transfers between devices with their start and end apart: 34 -> 38, of which waited for: 20 -> 10; matrix products, arithmetic and copies ran while one was open for 24% -> 17% of each run, Pallas kernels for 11% -> 34%
where the time goes in v2:
time: 497 us; the launch traced here: 492 us
  Pallas kernels  223 us (45%)
  matrix products  59.1 us (12%)
  waiting for transfers between devices  57.7 us (12%)
  local copies, waits for them, and re-layouts  56.6 us (11%)
  other arithmetic  47 us (9%)
  starting transfers between devices  46 us (9%)
    pallas_call x6, Pallas kernels, call(): pl.pallas_call(kernel, grid_spec=pltpu.PrefetchScalarGridSpec(num_scalar_...  168 us
    ppermute x20, waiting for transfers between devices, swap(): return lax.ppermute(value, axis, [(i, i ^ bit) for i in range(count)])  51.7 us
    pallas_call x1, Pallas kernels, feed_forward(): pl.pallas_call(functools.partial(up_kernel, chunk=chunk), grid=(tokens //...  30.8 us
    add x25, other arithmetic, add(): self.values.append(kept + got.astype(jnp.float32))  25.2 us
    pallas_call x1, Pallas kernels, feed_back(): pl.pallas_call(functools.partial(down_kernel, chunk=chunk), grid=(tokens...  24.1 us
    ppermute x20, starting transfers between devices, swap(): return lax.ppermute(value, axis, [(i, i ^ bit) for i in range(count)])  21.7 us
    unnamed x151, local copies, waits for them, and re-layouts  19 us
    ppermute x12, starting transfers between devices, slot_sends(): lax.ppermute(parts[shift], STREAM, turned(shift))  14.2 us
  transfers between devices with their start and end apart: 38, of which 10 were waited for; matrix products, arithmetic and copies ran while one was open for 17% of the time, Pallas kernels for 34%

profile of v2, /device:TPU:0, one launch (start us, length us, event | category | flops | bytes accessed | tf_op | source)
XLA Modules:
  0.0 491.8 jit_solution(15530338674492276661)
XLA Ops:
  3.4 5.0 %collective-permute-start = (bf16[2,128,768]{2,1,0:T(8,128)(2,1)}, bf16[2,128,768]{2,1,0:T(8,128)(2,1)S(1)}, u32[]{:S(2)}, u32[]{:S(2)}) collective-permute-start(bf16[2,128,768]{2,1,0:T(8,128)(2,1)} %get-tuple-element.286), channel_id=1, source_target_pairs={{0,3},{1,0},{2,1},{3,2},{4,7},{5,4},{6,5},{7,6},{8,11},{9,8},{10,9... | collective-permute-start | bytes 1179656 | tf_op jit(solution)/shard_map/ppermute | solution.py:512
  21.6 51.1 %make_bias.1 = (f32[16,12,192,256]{3,2,1,0:T(8,128)}, s32[16,192,256]{2,1,0:T(8,128)S(1)}) custom-call(s32[32]{0:T(128)S(1)} %reshape.184.bounds_ref, s32[2,576,128]{2,1,0:T(8,128)S(1)} %pad.26.col_ref, s32[2,8,640]{2,1,0:T(8,128)S(1)} %pad.25.row_ref, f32[12,128]{1,0:T(8,128)S(1)} %maximum_convert_fusion.1.plane_ref, f32[12,128]{1,0:T(8,128)S(1)} %pad.27.lines_ref), custom_call_target="tpu_custom_call" | custom-call | flops 30000001024 | bytes 30000000 | tf_op jit(solution)/shard_map/make_bias/pallas_call | solution.py:221
  78.6 4.0 collective-permute-start.3
  85.5 4.6 multiply_add_fusion
  93.1 6.0 %fusion = bf16[1152,2304]{1,0:T(8,128)(2,1)} fusion(bf16[1152,768]{1,0:T(8,128)(2,1)S(1)} %bitcast_convert_fusion.1, bf16[768,2304]{1,0:T(8,128)(2,1)S(1)} %copy-done.38, f32[2304]{0:T(1024)S(1)} %maximum_convert_fusion), kind=kOutput, calls=%fused_computation.2 | convolution fusion | flops 4082171904 | bytes 10626048 | tf_op jit(solution)/shard_map/dot_general | solution.py:638
  99.1 34.4 %attend.1 = (bf16[2,576,768]{2,1,0:T(8,128)(2,1)S(1)}, bf16[16,12,192,256]{3,2,1,0:T(8,128)(2,1)}) custom-call(s32[32]{0:T(128)S(1)} %reshape.184.bounds_ref, bf16[2,576,2304]{2,1,0:T(8,128)(2,1)} %bitcast.276, s32[2,8,640]{2,1,0:T(8,128)S(1)} %pad.25.row_ref, f32[16,12,192,256]{3,2,1,0:T(8,128)} %get-tuple-element.100.bias_ref), custom_call_target="tpu_custom_call" | custom-call | flops 20000000000 | bytes 20000000 | tf_op jit(solution)/shard_map/attend/pallas_call | solution.py:221
  137.5 30.8 %feed_forward.1 = (f32[1152,768]{1,0:T(8,128)}, bf16[1152,768]{1,0:T(8,128)(2,1)}, bf16[1152,3072]{1,0:T(8,128)(2,1)}, bf16[1152,3072]{1,0:T(8,128)(2,1)}, bf16[...) custom-call(bf16[1152,768]{1,0:T(8,128)(2,1)} %bitcast.256, ...), custom_call_target="tpu_custom_call" | custom-call | flops 20000000000 | bytes 60000000 | tf_op jit(solution)/shard_map/feed_forward/pallas_call | solution.py:388
  168.3 9.6 %fusion.64 = f32[3072,768]{1,0:T(8,128)S(1)} fusion(bf16[1152,3072]{1,0:T(8,128)(2,1)} %get-tuple-element.105, bf16[1152,768]{1,0:T(8,128)(2,1)} %get-tuple-element.112.branch_ref), kind=kOutput, calls=%fused_computation.218 | convolution fusion | flops 5435817984 | bytes 18284544 | tf_op jit(solution)/shard_map/tf,td->fd/dot_general | solution.py:647
  192.2 24.1 %feed_back.1 = (bf16[1152,3072]{1,0:T(8,128)(2,1)}, f32[1152,768]{1,0:T(8,128)}, bf16[1152,768]{1,0:T(8,128)(2,1)}, bf16[1152,768]{1,0:T(8,128)(2,1)}, f32[8,768]{1,0:T(8,128)}, /*index=5*/f32[8,3072]{1,0:T(8,128)}) custom-call(bf16[1152,768]{1,0:T(8,128)(2,1)} %get-tuple-element.112.branch_ref, bf16[1152,3072]{1,0:T(8,128)(2,1)} %get-tuple-element.113.slope_ref, ...), custom_call_target="tpu_custom_call" | custom-call | flops 20000000000 | bytes 60000000 | tf_op jit(solution)/shard_map/feed_back/pallas_call | solution.py:407
  216.3 9.4 %fusion.66 = f32[768,3072]{1,0:T(8,128)S(1)} fusion(bf16[1152,768]{1,0:T(8,128)(2,1)} %get-tuple-element.118, bf16[1152,3072]{1,0:T(8,128)(2,1)} %get-tuple-element.119), kind=kOutput, calls=%fused_computation.220 | convolution fusion | flops 5435817984 | bytes 18284544 | tf_op jit(solution)/shard_map/td,tf->df/dot_general | solution.py:660
  243.0 17.9 %attend_back.2 = (bf16[1,576,2304]{2,1,0:T(8,128)(2,1)S(1)}, bf16[8,12,192,256]{3,2,1,0:T(8,128)(2,1)}) custom-call(s32[32]{0:T(128)S(1)} %reshape.184.bounds_ref, bf16[2,576,2304]{2,1,0:T(8,128)(2,1)} %bitcast.277, bf16[2,576,768]{2,1,0:T(8,128)(2,1)S(1)} %bitcast.258, bf16[16,12,192,256]{3,2,1,0:T(8,128)(2,1)} %get-tuple-element.132.shares_ref), custom_call_target="tpu_custom_call" | custom-call | flops 12000000000 | bytes 12000000 | tf_op jit(solution)/shard_map/attend_back/pallas_call | solution.py:221
  268.0 6.0 %collective-permute-start.18 = (bf16[2,2,96,768]{3,2,0,1:T(8,128)(2,1)}, bf16[2,2,96,768]{3,2,0,1:T(8,128)(2,1)}, u32[]{:S(2)}, u32[]{:S(2)}) collective-permute-start(bf16[2,2,96,768]{3,2,0,1:T(8,128)(2,1)} %fusion.24), channel_id=1, source_target_pairs={{0,16},{4,20},{8,24},{12,28},{16,0},{20,4},{24,8},{28,12},{1,17},{... | collective-permute-start | bytes 1769480 | tf_op jit(solution)/shard_map/ppermute | solution.py:427
  274.0 5.1 %fusion.22 = f32[768,2304]{1,0:T(8,128)} fusion(bf16[576,2304]{1,0:T(8,128)(2,1)S(1)} %bitcast.253, bf16[1152,768]{1,0:T(8,128)(2,1)S(1)} %copy-done.13), kind=kOutput, calls=%fused_computation.60 | convolution fusion | flops 2038431744 | bytes 10616832 | tf_op jit(solution)/shard_map/td,te->de/dot_general | solution.py:683
  287.2 17.9 %attend_back.3 = (bf16[1,576,2304]{2,1,0:T(8,128)(2,1)S(1)}, bf16[8,12,192,256]{3,2,1,0:T(8,128)(2,1)}) custom-call(s32[32]{0:T(128)S(1)} %reshape.184.bounds_ref, bf16[2,576,2304]{2,1,0:T(8,128)(2,1)} %bitcast.278, bf16[2,576,768]{2,1,0:T(8,128)(2,1)S(1)} %bitcast.259, bf16[16,12,192,256]{3,2,1,0:T(8,128)(2,1)} %get-tuple-element.132.shares_ref), custom_call_target="tpu_custom_call" | custom-call | flops 12000000000 | bytes 12000000 | tf_op jit(solution)/shard_map/attend_back/pallas_call | solution.py:221
  306.5 12.3 %collective-permute-done.19 = bf16[2,2,2,24,3840]{4,3,1,2,0:T(8,128)(2,1)} collective-permute-done((bf16[2,2,2,24,3840]{4,3,1,2,0:T(8,128)(2,1)S(1)}, bf16[2,2,2,24,3840]{4,3,1,2,0:T(8,128)(2,1)}, u32[]{:S(2)}, u32[]{:S(2)}) %collective-permute-start.19) | collective-permute-done | bytes 1474592 | tf_op jit(solution)/shard_map/ppermute | solution.py:427
  339.9 5.2 %convolution_add_fusion.1 = f32[768,2304]{1,0:T(8,128)S(1)} fusion(f32[768,2304]{1,0:T(8,128)} %fusion.22, bf16[576,2304]{1,0:T(8,128)(2,1)S(1)} %bitcast.251, bf16[1152,768]{1,0:T(8,128)(2,1)S(1)} %copy-done.14), kind=kOutput, calls=%fused_computation.3 | convolution fusion | flops 2040201216 | bytes 17694720 | tf_op jit(solution)/shard_map/td,te->de/dot_general | solution.py:683
  360.3 24.0 %make_bins.2 = f32[16,768]{1,0:T(8,128)S(1)} custom-call(s32[32]{0:T(128)S(1)} %reshape.184.bounds_ref, s32[16,192,256]{2,1,0:T(8,128)S(1)} %copy-done.5, bf16[8,12,192,256]{3,2,1,0:T(8,128)(2,1)} %get-tuple-element.151.ds_ref), custom_call_target="tpu_custom_call" | custom-call | flops 12000000000 | bytes 12000000 | tf_op jit(solution)/shard_map/make_bins/pallas_call | solution.py:221
  388.7 5.8 %collective-permute-done.20 = bf16[128,768]{1,0:T(8,128)(2,1)S(1)} collective-permute-done((bf16[128,768]{1,0:T(8,128)(2,1)S(1)}, bf16[128,768]{1,0:T(8,128)(2,1)S(1)}, u32[]{:S(2)}, u32[]{:S(2)}) %collective-permute-start.20) | collective-permute-done | bytes 196640 | tf_op jit(solution)/shard_map/ppermute | solution.py:520
  400.3 22.2 %make_bins.3 = f32[16,768]{1,0:T(8,128)S(1)} custom-call(s32[32]{0:T(128)S(1)} %reshape.184.bounds_ref, s32[16,192,256]{2,1,0:T(8,128)S(1)} %copy-done.5, bf16[8,12,192,256]{3,2,1,0:T(8,128)(2,1)} %get-tuple-element.162.ds_ref), custom_call_target="tpu_custom_call" | custom-call | flops 12000000000 | bytes 12000000 | tf_op jit(solution)/shard_map/make_bins/pallas_call | solution.py:221
  430.3 6.6 %collective-permute-done.27 = bf16[2,24,3840]{2,1,0:T(8,128)(2,1)S(1)} collective-permute-done((bf16[2,24,3840]{2,1,0:T(8,128)(2,1)S(1)}, bf16[2,24,3840]{2,1,0:T(8,128)(2,1)S(1)}, u32[]{:S(2)}, u32[]{:S(2)}) %collective-permute-start.27) | collective-permute-done | bytes 368672 | tf_op jit(solution)/shard_map/ppermute | solution.py:427
  436.9 10.0 %collective-permute-done.28 = bf16[2,2,2,24,2560]{4,3,2,1,0:T(8,128)(2,1)S(1)} collective-permute-done((bf16[2,2,2,24,2560]{4,3,2,1,0:T(8,128)(2,1)S(1)}, bf16[2,2,2,24,2560]{4,3,2,1,0:T(8,128)(2,1)S(1)}, u32[]{:S(2)}, u32[]{:S(2)}) %collective-permute-start.28) | collective-permute-done | bytes 983072 | tf_op jit(solution)/shard_map/ppermute | solution.py:427
  461.0 7.8 %collective-permute-done.34 = f32[40,768]{1,0:T(8,128)S(1)} collective-permute-done((f32[40,768]{1,0:T(8,128)S(1)}, f32[40,768]{1,0:T(8,128)S(1)}, u32[]{:S(2)}, u32[]{:S(2)}) %collective-permute-start.34) | collective-permute-done | bytes 122912 | tf_op jit(solution)/shard_map/ppermute | solution.py:427
  477.3 5.8 %collective-permute-done.36 = f32[40,768]{1,0:T(8,128)S(1)} collective-permute-done((f32[40,768]{1,0:T(8,128)S(1)}, f32[40,768]{1,0:T(8,128)S(1)}, u32[]{:S(2)}, u32[]{:S(2)}) %collective-permute-start.36) | collective-permute-done | bytes 122912 | tf_op jit(solution)/shard_map/ppermute | solution.py:427
  485.9 4.2 collective-permute-done.31
  (381 shorter events, 158.9 us)
Async XLA Ops:
  3.4 71.6 %collective-permute-start = (bf16[2,128,768]{2,1,0:T(8,128)(2,1)}, bf16[2,128,768]{2,1,0:T(8,128)(2,1)S(1)}, u32[]{:S(2)}, u32[]{:S(2)}) collective-permute-start(bf16[2,128,768]{2,1,0:T(8,128)(2,1)} %get-tuple-element.286), channel_id=1, source_target_pairs={{0,3},{1,0},{2,1},{3,2},{4,7},{5,4},{6,5},{7,6},{8,11},{9,8},{10,9... | collective-permute-start | bytes 1179656 | tf_op jit(solution)/shard_map/ppermute | solution.py:512
  8.4 66.5 %collective-permute-start.2 = (bf16[2,128,768]{2,1,0:T(8,128)(2,1)}, bf16[2,128,768]{2,1,0:T(8,128)(2,1)S(1)}, u32[]{:S(2)}, u32[]{:S(2)}) collective-permute-start(bf16[2,128,768]{2,1,0:T(8,128)(2,1)} %get-tuple-element.287), channel_id=1, source_target_pairs={{0,1},{1,2},{2,3},{3,0},{4,5},{5,6},{6,7},{7,4},{8,9},{9,10},{10,1... | collective-permute-start | bytes 1179656 | tf_op jit(solution)/shard_map/ppermute | solution.py:512
  8.4 66.5 %collective-permute-start.1 = (bf16[2,128,768]{2,1,0:T(8,128)(2,1)}, bf16[2,128,768]{2,1,0:T(8,128)(2,1)}, u32[]{:S(2)}, u32[]{:S(2)}) collective-permute-start(bf16[2,128,768]{2,1,0:T(8,128)(2,1)} %get-tuple-element.288), channel_id=1, source_target_pairs={{0,2},{1,3},{2,0},{3,1},{4,6},{5,7},{6,4},{7,5},{8,10},{9,11},{10,... | collective-permute-start | bytes 1179656 | tf_op jit(solution)/shard_map/ppermute | solution.py:512
  78.6 55.0 %collective-permute-start.5 = (bf16[2,128,768]{2,1,0:T(8,128)(2,1)}, bf16[2,128,768]{2,1,0:T(8,128)(2,1)S(1)}, u32[]{:S(2)}, u32[]{:S(2)}) collective-permute-start(bf16[2,128,768]{2,1,0:T(8,128)(2,1)} %get-tuple-element.282), channel_id=1, source_target_pairs={{0,1},{1,2},{2,3},{3,0},{4,5},{5,6},{6,7},{7,4},{8,9},{9,10},{10,1... | collective-permute-start | bytes 1179656 | tf_op jit(solution)/shard_map/ppermute | solution.py:512
  78.6 55.0 %collective-permute-start.4 = (bf16[2,128,768]{2,1,0:T(8,128)(2,1)}, bf16[2,128,768]{2,1,0:T(8,128)(2,1)S(1)}, u32[]{:S(2)}, u32[]{:S(2)}) collective-permute-start(bf16[2,128,768]{2,1,0:T(8,128)(2,1)} %get-tuple-element.283), channel_id=1, source_target_pairs={{0,2},{1,3},{2,0},{3,1},{4,6},{5,7},{6,4},{7,5},{8,10},{9,11},{10,... | collective-permute-start | bytes 1179656 | tf_op jit(solution)/shard_map/ppermute | solution.py:512
  78.6 55.0 %collective-permute-start.3 = (bf16[2,128,768]{2,1,0:T(8,128)(2,1)S(1)}, bf16[2,128,768]{2,1,0:T(8,128)(2,1)S(1)}, u32[]{:S(2)}, u32[]{:S(2)}) collective-permute-start(bf16[2,128,768]{2,1,0:T(8,128)(2,1)S(1)} %get-tuple-element.284), channel_id=1, source_target_pairs={{0,3},{1,0},{2,1},{3,2},{4,7},{5,4},{6,5},{7,6},{8,11},{9,8},{10,9... | collective-permute-start | bytes 1179656 | tf_op jit(solution)/shard_map/ppermute | solution.py:512
  187.2 40.3 %collective-permute-start.12 = (bf16[128,768]{1,0:T(8,128)(2,1)}, bf16[128,768]{1,0:T(8,128)(2,1)}, u32[]{:S(2)}, u32[]{:S(2)}) collective-permute-start(bf16[128,768]{1,0:T(8,128)(2,1)} %get-tuple-element.273), channel_id=1, source_target_pairs={{0,3},{1,0},{2,1},{3,2},{4,7},{5,4},{6,5},{7,6},{8,11},{9,8},{10,9... | collective-permute-start | bytes 589832 | tf_op jit(solution)/shard_map/ppermute | solution.py:520
  187.2 46.1 %collective-permute-start.11 = (bf16[128,768]{1,0:T(8,128)(2,1)}, bf16[128,768]{1,0:T(8,128)(2,1)}, u32[]{:S(2)}, u32[]{:S(2)}) collective-permute-start(bf16[128,768]{1,0:T(8,128)(2,1)} %get-tuple-element.274), channel_id=1, source_target_pairs={{0,2},{1,3},{2,0},{3,1},{4,6},{5,7},{6,4},{7,5},{8,10},{9,11},{10,... | collective-permute-start | bytes 589832 | tf_op jit(solution)/shard_map/ppermute | solution.py:520
  188.2 47.3 %collective-permute-start.10 = (bf16[128,768]{1,0:T(8,128)(2,1)}, bf16[128,768]{1,0:T(8,128)(2,1)}, u32[]{:S(2)}, u32[]{:S(2)}) collective-permute-start(bf16[128,768]{1,0:T(8,128)(2,1)} %get-tuple-element.275), channel_id=1, source_target_pairs={{0,1},{1,2},{2,3},{3,0},{4,5},{5,6},{6,7},{7,4},{8,9},{9,10},{10,1... | collective-permute-start | bytes 589832 | tf_op jit(solution)/shard_map/ppermute | solution.py:520
  190.2 45.3 %collective-permute-start.9 = (bf16[128,768]{1,0:T(8,128)(2,1)}, bf16[128,768]{1,0:T(8,128)(2,1)}, u32[]{:S(2)}, u32[]{:S(2)}) collective-permute-start(bf16[128,768]{1,0:T(8,128)(2,1)} %get-tuple-element.277), channel_id=1, source_target_pairs={{0,3},{1,0},{2,1},{3,2},{4,7},{5,4},{6,5},{7,6},{8,11},{9,8},{10,9... | collective-permute-start | bytes 589832 | tf_op jit(solution)/shard_map/ppermute | solution.py:520
  192.0 43.5 %collective-permute-start.8 = (bf16[128,768]{1,0:T(8,128)(2,1)}, bf16[128,768]{1,0:T(8,128)(2,1)}, u32[]{:S(2)}, u32[]{:S(2)}) collective-permute-start(bf16[128,768]{1,0:T(8,128)(2,1)} %get-tuple-element.278), channel_id=1, source_target_pairs={{0,2},{1,3},{2,0},{3,1},{4,6},{5,7},{6,4},{7,5},{8,10},{9,11},{10,... | collective-permute-start | bytes 589832 | tf_op jit(solution)/shard_map/ppermute | solution.py:520
  233.4 27.6 %collective-permute-start.13 = (bf16[2,2,2,96,768]{4,3,1,2,0:T(8,128)(2,1)}, bf16[2,2,2,96,768]{4,3,1,2,0:T(8,128)(2,1)}, u32[]{:S(2)}, u32[]{:S(2)}) collective-permute-start(bf16[2,2,2,96,768]{4,3,1,2,0:T(8,128)(2,1)} %fusion.18), channel_id=1, source_target_pairs={{0,8},{4,12},{8,0},{12,4},{16,24},{20,28},{24,16},{28,20},{1,9},{5... | collective-permute-start | bytes 3538952 | tf_op jit(solution)/shard_map/ppermute | solution.py:427
  236.4 24.6 %collective-permute-start.14 = (bf16[2,2,2,2,24,3840]{5,4,2,3,1,0:T(8,128)(2,1)S(1)}, bf16[2,2,2,2,24,3840]{5,4,2,3,1,0:T(8,128)(2,1)S(1)}, u32[]{:S(2)}, u32[]{:S(2)}) collective-permute-start(bf16[2,2,2,2,24,3840]{5,4,2,3,1,0:T(8,128)(2,1)S(1)} %pad_maximum_fusion), channel_id=1, source_target_pairs={{0,4},{4,0},{8,12},{12,8},{16,20},{20,16},{24,28},{28,24},{1,5},{5... | collective-permute-start | bytes 8847368 | tf_op jit(solution)/shard_map/ppermute | solution.py:427
  268.0 38.5 %collective-permute-start.18 = (bf16[2,2,96,768]{3,2,0,1:T(8,128)(2,1)}, bf16[2,2,96,768]{3,2,0,1:T(8,128)(2,1)}, u32[]{:S(2)}, u32[]{:S(2)}) collective-permute-start(bf16[2,2,96,768]{3,2,0,1:T(8,128)(2,1)} %fusion.24), channel_id=1, source_target_pairs={{0,16},{4,20},{8,24},{12,28},{16,0},{20,4},{24,8},{28,12},{1,17},{... | collective-permute-start | bytes 1769480 | tf_op jit(solution)/shard_map/ppermute | solution.py:427
  282.5 24.0 %collective-permute-start.17 = (bf16[128,768]{1,0:T(8,128)(2,1)S(1)}, bf16[128,768]{1,0:T(8,128)(2,1)}, u32[]{:S(2)}, u32[]{:S(2)}) collective-permute-start(bf16[128,768]{1,0:T(8,128)(2,1)S(1)} %get-tuple-element.293), channel_id=1, source_target_pairs={{0,3},{1,0},{2,1},{3,2},{4,7},{5,4},{6,5},{7,6},{8,11},{9,8},{10,9... | collective-permute-start | bytes 589832 | tf_op jit(solution)/shard_map/ppermute | solution.py:520
  284.3 22.2 %collective-permute-start.16 = (bf16[128,768]{1,0:T(8,128)(2,1)S(1)}, bf16[128,768]{1,0:T(8,128)(2,1)}, u32[]{:S(2)}, u32[]{:S(2)}) collective-permute-start(bf16[128,768]{1,0:T(8,128)(2,1)S(1)} %get-tuple-element.294), channel_id=1, source_target_pairs={{0,2},{1,3},{2,0},{3,1},{4,6},{5,7},{6,4},{7,5},{8,10},{9,11},{10,... | collective-permute-start | bytes 589832 | tf_op jit(solution)/shard_map/ppermute | solution.py:520
  284.7 21.9 %collective-permute-start.15 = (bf16[128,768]{1,0:T(8,128)(2,1)S(1)}, bf16[128,768]{1,0:T(8,128)(2,1)}, u32[]{:S(2)}, u32[]{:S(2)}) collective-permute-start(bf16[128,768]{1,0:T(8,128)(2,1)S(1)} %get-tuple-element.295), channel_id=1, source_target_pairs={{0,1},{1,2},{2,3},{3,0},{4,5},{5,6},{6,7},{7,4},{8,9},{9,10},{10,1... | collective-permute-start | bytes 589832 | tf_op jit(solution)/shard_map/ppermute | solution.py:520
  287.1 31.8 %collective-permute-start.19 = (bf16[2,2,2,24,3840]{4,3,1,2,0:T(8,128)(2,1)S(1)}, bf16[2,2,2,24,3840]{4,3,1,2,0:T(8,128)(2,1)}, u32[]{:S(2)}, u32[]{:S(2)}) collective-permute-start(bf16[2,2,2,24,3840]{4,3,1,2,0:T(8,128)(2,1)S(1)} %pad_maximum_fusion.4), channel_id=1, source_target_pairs={{0,16},{4,20},{8,24},{12,28},{16,0},{20,4},{24,8},{28,12},{1,17},{... | collective-permute-start | bytes 4423688 | tf_op jit(solution)/shard_map/ppermute | solution.py:427
  350.4 44.0 %collective-permute-start.23 = (bf16[2,96,768]{2,1,0:T(8,128)(2,1)}, bf16[2,96,768]{2,1,0:T(8,128)(2,1)}, u32[]{:S(2)}, u32[]{:S(2)}) collective-permute-start(bf16[2,96,768]{2,1,0:T(8,128)(2,1)} %fusion.34), channel_id=1, source_target_pairs={{0,1},{1,0},{2,3},{3,2},{4,5},{5,4},{6,7},{7,6},{8,9},{9,8},{10,11... | collective-permute-start | bytes 884744 | tf_op jit(solution)/shard_map/ppermute | solution.py:427
  353.1 41.3 %collective-permute-start.24 = (bf16[2,2,24,3840]{3,2,0,1:T(8,128)(2,1)}, bf16[2,2,24,3840]{3,2,0,1:T(8,128)(2,1)}, u32[]{:S(2)}, u32[]{:S(2)}) collective-permute-start(bf16[2,2,24,3840]{3,2,0,1:T(8,128)(2,1)} %pad_maximum_fusion.6), channel_id=1, source_target_pairs={{0,8},{4,12},{8,0},{12,4},{16,24},{20,28},{24,16},{28,20},{1,9},{5... | collective-permute-start | bytes 2211848 | tf_op jit(solution)/shard_map/ppermute | solution.py:427
  354.3 32.5 %collective-permute-start.22 = (bf16[128,768]{1,0:T(8,128)(2,1)}, bf16[128,768]{1,0:T(8,128)(2,1)}, u32[]{:S(2)}, u32[]{:S(2)}) collective-permute-start(bf16[128,768]{1,0:T(8,128)(2,1)} %get-tuple-element.289), channel_id=1, source_target_pairs={{0,3},{1,0},{2,1},{3,2},{4,7},{5,4},{6,5},{7,6},{8,11},{9,8},{10,9... | collective-permute-start | bytes 589832 | tf_op jit(solution)/shard_map/ppermute | solution.py:520
  356.6 32.1 %collective-permute-start.21 = (bf16[128,768]{1,0:T(8,128)(2,1)}, bf16[128,768]{1,0:T(8,128)(2,1)}, u32[]{:S(2)}, u32[]{:S(2)}) collective-permute-start(bf16[128,768]{1,0:T(8,128)(2,1)} %get-tuple-element.290), channel_id=1, source_target_pairs={{0,2},{1,3},{2,0},{3,1},{4,6},{5,7},{6,4},{7,5},{8,10},{9,11},{10,... | collective-permute-start | bytes 589832 | tf_op jit(solution)/shard_map/ppermute | solution.py:520
  358.3 36.1 %collective-permute-start.25 = (bf16[2,2,2,2,24,2560]{5,4,3,2,1,0:T(8,128)(2,1)}, bf16[2,2,2,2,24,2560]{5,4,3,2,1,0:T(8,128)(2,1)}, u32[]{:S(2)}, u32[]{:S(2)}) collective-permute-start(bf16[2,2,2,2,24,2560]{5,4,3,2,1,0:T(8,128)(2,1)} %pad_maximum_fusion.1), channel_id=1, source_target_pairs={{0,4},{4,0},{8,12},{12,8},{16,20},{20,16},{24,28},{28,24},{1,5},{5... | collective-permute-start | bytes 5898248 | tf_op jit(solution)/shard_map/ppermute | solution.py:427
  424.7 22.1 %collective-permute-start.28 = (bf16[2,2,2,24,2560]{4,3,2,1,0:T(8,128)(2,1)S(1)}, bf16[2,2,2,24,2560]{4,3,2,1,0:T(8,128)(2,1)S(1)}, u32[]{:S(2)}, u32[]{:S(2)}) collective-permute-start(bf16[2,2,2,24,2560]{4,3,2,1,0:T(8,128)(2,1)S(1)} %pad_maximum_fusion.5), channel_id=1, source_target_pairs={{0,8},{4,12},{8,0},{12,4},{16,24},{20,28},{24,16},{28,20},{1,9},{5... | collective-permute-start | bytes 2949128 | tf_op jit(solution)/shard_map/ppermute | solution.py:427
  (85 other events, 1137.6 us)
